TPU v7x, 128 devices: a whole 4x4x4 slice. The times are simulated.
128 devices in a mesh: az: 32 (over z, y_lo, x), rad: 4 (over y_hi, core).
Axes of the slice: x: 4, y: 4 (y_hi: 2, y_lo: 2; y = y_hi * 2 + y_lo), z: 4, core: 2. Of those that a mesh axis runs over, the one named last changes fastest.
Arguments:
- state: bfloat16 [4, 64, 2048, 512], P(None, None, 'az', 'rad'), may hold values from -6 to 6
- source: bfloat16 [64, 2048, 512], P(None, 'az', 'rad'), may hold values from -6 to 6
- shear: bfloat16 [64, 2048, 512], P(None, 'az', 'rad'), may hold values from 0.5 to 4
- permeability: bfloat16 [64, 2048, 512], P(None, 'az', 'rad'), may hold values from 0.099609375 to 10
- radial_basis: float32 [512, 512], P('rad'), may hold values from -1 to 2
- radial_eigen: float32 [512], replicated, may hold values from 4e-05 to 4
Outputs:
- correction: bfloat16 [4, 64, 2048, 512], P(None, None, 'az', 'rad')
All inputs are finite; a program needn't handle non-finite values.
Results may differ from a plain program's by a relative error of at most 0.001.
Values may be sent and summed in bfloat16 or wider, within the bound.
A program may use at most 192 MiB of HBM per device.

v0:
```python
import math

import jax
import jax.numpy as jnp
from jax import lax
from jax.sharding import PartitionSpec as P

NH = 64


biot_coupling = 2.0
storage = 1.0


def padded_2(cells, sides, width):
    for axis, dim in sides:
        count = lax.axis_size(axis)
        head = lax.slice_in_dim(cells, 0, width, axis=dim)
        tail = lax.slice_in_dim(cells, cells.shape[dim] - width, cells.shape[dim], axis=dim)
        cells = jnp.concatenate(
            [
                lax.ppermute(tail, axis, [(i, (i + 1) % count) for i in range(count)]),
                cells,
                lax.ppermute(head, axis, [((i + 1) % count, i) for i in range(count)]),
            ],
            axis=dim,
        )
    return cells


def contract(form, left, right):
    return jnp.einsum(
        form, left, right, precision=lax.Precision.HIGHEST, preferred_element_type=jnp.float32
    )


def neighbor(extended, grid_axis, offset):
    lead = extended.ndim - 3
    window = [slice(None)] * lead + [slice(1, -1)] * 3
    length = extended.shape[lead + grid_axis]
    window[lead + grid_axis] = slice(1 + offset, length - 1 + offset)
    return extended[tuple(window)]


def stencil(extended, source_block):
    center = neighbor(extended, 0, 0)
    diagonal = jnp.zeros_like(center[4])
    momentum = [jnp.zeros_like(center[0]), jnp.zeros_like(center[0]), jnp.zeros_like(center[0])]
    fluid = jnp.zeros_like(center[0])
    for grid_axis in (0, 1, 2):
        for offset in (1, -1):
            beside = neighbor(extended, grid_axis, offset)
            shear_face = 0.5 * (center[4] + beside[4])
            flow_face = 0.5 * (center[5] + beside[5])
            diagonal = diagonal + shear_face
            momentum = [
                momentum[channel] + shear_face * (center[channel] - beside[channel])
                for channel in range(3)
            ]
            fluid = fluid + flow_face * (center[3] - beside[3])
    component_axes = (2, 1, 0)
    pressure = extended[3]
    spread = jnp.zeros_like(center[0])
    parts = []
    for channel in range(3):
        grid_axis = component_axes[channel]
        gradient = 0.5 * (neighbor(pressure, grid_axis, 1) - neighbor(pressure, grid_axis, -1))
        parts.append(-(momentum[channel] + biot_coupling * gradient))
        member = extended[channel]
        spread = spread + 0.5 * (neighbor(member, grid_axis, 1) - neighbor(member, grid_axis, -1))
    parts.append(source_block + biot_coupling * spread + storage * center[3] + fluid)
    return (jnp.stack(parts), diagonal)


def cosine_table(extent):
    row_ids = jnp.arange(extent, dtype=jnp.float32)[:, None]
    col_ids = jnp.arange(extent, dtype=jnp.float32)[None, :]
    scaled = jnp.where(row_ids == 0, math.sqrt(1.0 / extent), math.sqrt(2.0 / extent))
    return scaled * jnp.cos(math.pi * (col_ids + 0.5) * row_ids / extent)


def fourier_pair(rows_len, cols_len, period):
    row_ids = jnp.arange(rows_len, dtype=jnp.int32)[:, None]
    col_ids = jnp.arange(cols_len, dtype=jnp.int32)[None, :]
    angle = 2.0 * math.pi / period * (row_ids * col_ids % period).astype(jnp.float32)
    return (jnp.cos(angle), jnp.sin(angle))


def spectral_solve(coeffs, mode_start, radial_eigen):
    moved = lax.all_to_all(coeffs, "az", split_axis=0, concat_axis=2, tiled=True)
    mode_count, level_count, length = moved.shape
    inner_len = 128
    outer_len = length // inner_len
    lines = moved.reshape(mode_count, level_count, outer_len, inner_len)
    cos_outer, sin_outer = fourier_pair(outer_len, outer_len, outer_len)
    cos_inner, sin_inner = fourier_pair(inner_len, inner_len, inner_len)
    tw_cos, tw_sin = fourier_pair(outer_len, inner_len, length)
    real_one = contract("mlab,ak->mlkb", lines, cos_outer)
    imag_one = -contract("mlab,ak->mlkb", lines, sin_outer)
    turned_real = real_one * tw_cos + imag_one * tw_sin
    turned_imag = imag_one * tw_cos - real_one * tw_sin
    spec_real = contract("mlkb,bj->mlkj", turned_real, cos_inner) + contract(
        "mlkb,bj->mlkj", turned_imag, sin_inner
    )
    spec_imag = contract("mlkb,bj->mlkj", turned_imag, cos_inner) - contract(
        "mlkb,bj->mlkj", turned_real, sin_inner
    )
    mode_eigen = lax.dynamic_slice_in_dim(radial_eigen, mode_start, mode_count)
    levels = jnp.arange(level_count, dtype=jnp.int32).astype(jnp.float32)
    height_eigen = 4.0 * jnp.sin(math.pi * levels / (2.0 * NH)) ** 2
    first_ids = jnp.arange(outer_len, dtype=jnp.float32)[:, None]
    second_ids = jnp.arange(inner_len, dtype=jnp.float32)[None, :]
    waves = first_ids + outer_len * second_ids
    azimuth_eigen = 4.0 * jnp.sin(math.pi * waves / length) ** 2
    totals = (
        storage
        + mode_eigen[:, None, None, None]
        + height_eigen[None, :, None, None]
        + azimuth_eigen[None, None, :, :]
    )
    solved_real = spec_real / totals
    solved_imag = spec_imag / totals
    back_real = contract("mlkj,bj->mlkb", solved_real, cos_inner) - contract(
        "mlkj,bj->mlkb", solved_imag, sin_inner
    )
    back_imag = contract("mlkj,bj->mlkb", solved_imag, cos_inner) + contract(
        "mlkj,bj->mlkb", solved_real, sin_inner
    )
    untwist_real = back_real * tw_cos - back_imag * tw_sin
    untwist_imag = back_imag * tw_cos + back_real * tw_sin
    signal = contract("mlkb,ak->mlab", untwist_real, cos_outer) - contract(
        "mlkb,ak->mlab", untwist_imag, sin_outer
    )
    signal = (signal * (1.0 / length)).reshape(mode_count, level_count, length)
    return lax.all_to_all(signal, "az", split_axis=2, concat_axis=0, tiled=True)


def precondition(residual_p, radial_basis, radial_eigen):
    cosine = cosine_table(NH)
    heights = contract("lh,har->lar", cosine, residual_p)
    local_radii = heights.shape[2]
    columns = radial_basis
    coeffs = lax.psum_scatter(
        contract("lar,rm->mla", heights, columns), "rad", scatter_dimension=0, tiled=True
    )
    mode_start = lax.axis_index("rad") * local_radii + lax.axis_index("az") * (
        local_radii // lax.axis_size("az")
    )
    solved = spectral_solve(coeffs, mode_start, radial_eigen)
    columns = radial_basis
    planes = contract("mla,rm->lar", lax.all_gather(solved, "rad", axis=0, tiled=True), columns)
    return contract("lh,lar->har", cosine, planes)


def body(state, source, shear, permeability, radial_basis, radial_eigen):
    stacked = jnp.concatenate([state, shear[None], permeability[None]], axis=0)
    padded = padded_2(stacked, (("az", 2), ("rad", 3)), 1)
    rad_count = lax.axis_size("rad")
    rad_place = lax.axis_index("rad")
    column = lax.broadcasted_iota(jnp.int32, (padded.shape[3],), 0)
    outside = (column == 0) & (rad_place == 0) | (column == padded.shape[3] - 1) & (
        rad_place == rad_count - 1
    )
    padded = jnp.where(outside, jnp.zeros((), padded.dtype), padded)
    extended = jnp.pad(padded.astype(jnp.float32), ((0, 0), (1, 1), (0, 0), (0, 0)))
    residual, diagonal = stencil(extended, source.astype(jnp.float32))
    moment_step = residual[:3] / diagonal
    press_step = precondition(residual[3], radial_basis, radial_eigen)
    local_rr = jnp.sum(residual * residual)
    local_rz = jnp.sum(residual[:3] * moment_step) + jnp.sum(residual[3] * press_step)
    total_rr, total_rz = lax.psum((local_rr, local_rz), ("az", "rad"))
    alpha = total_rr / total_rz
    return jnp.concatenate(
        [
            (alpha * moment_step).astype(jnp.bfloat16),
            (alpha * press_step).astype(jnp.bfloat16)[None],
        ],
        axis=0,
    )


def solution(mesh):
    placed = (
        P(None, None, "az", "rad"),
        P(None, "az", "rad"),
        P(None, "az", "rad"),
        P(None, "az", "rad"),
        P("rad", None),
        P(),
    )
    return jax.shard_map(
        body, mesh=mesh, in_specs=placed, out_specs=P(None, None, "az", "rad"), check_vma=False
    )
```

profile of v0, /device:TPU:1, one launch (start us, length us, event | category | flops | bytes accessed | tf_op | source)
XLA Modules:
  0.0 562.8 jit_solution(13840592234167820502)
XLA Ops:
  6.5 5.0 copy.39
  13.7 7.9 %collective-permute-start.1 = (bf16[6,64,1,128]{3,1,2,0:T(8,128)(2,1)S(1)}, bf16[6,64,1,128]{3,1,2,0:T(8,128)(2,1)S(1)}, u32[]{:S(2)}, u32[]{:S(2)}) collective-permute-start(bf16[6,64,1,128]{3,1,2,0:T(8,128)(2,1)S(1)} %get-tuple-element.21), channel_id=1, source_target_pairs={{4,0},{8,4},{12,8},{16,12},{20,16},{24,20},{28,24},{32,28},{36,32}... | collective-permute-start | bytes 294920 | tf_op jit(solution)/shard_map/ppermute | solution.py:24
  23.2 6.0 %collective-permute-done = bf16[6,64,1,128]{3,1,2,0:T(8,128)(2,1)S(1)} collective-permute-done((bf16[6,64,1,128]{3,1,2,0:T(8,128)(2,1)S(1)}, bf16[6,64,1,128]{3,1,2,0:T(8,128)(2,1)S(1)}, u32[]{:S(2)}, u32[]{:S(2)}) %collective-permute-start) | collective-permute-done | bytes 98336 | tf_op jit(solution)/shard_map/ppermute | solution.py:22
  29.2 3.9 pad_maximum_fusion
  33.1 6.4 %fusion.237 = (bf16[6,64,66,1]{3,1,2,0:T(8,128)(2,1)}, bf16[6,64,66,1]{3,1,2,0:T(8,128)(2,1)}) fusion(bf16[6,64,66,128]{3,1,2,0:T(8,128)(2,1)S(1)} %pad_maximum_fusion), kind=kLoop, calls=%fused_computation.305 | loop fusion | bytes 202752 | tf_op jit(solution)/shard_map/slice | solution.py:19
  39.5 8.5 %copy.41 = bf16[6,64,66,1]{2,1,3,0:T(8,128)(2,1)S(1)} copy(bf16[6,64,66,1]{3,1,2,0:T(8,128)(2,1)} %get-tuple-element.19) | data formatting | bytes 101376 | tf_op jit(solution)/shard_map/slice | solution.py:18
  47.9 2.2 collective-permute-start.3
  50.1 8.5 %copy.40 = bf16[6,64,66,1]{2,1,3,0:T(8,128)(2,1)S(1)} copy(bf16[6,64,66,1]{3,1,2,0:T(8,128)(2,1)} %get-tuple-element.18) | data formatting | bytes 101376 | tf_op jit(solution)/shard_map/slice | solution.py:19
  58.6 2.8 collective-permute-start.2
  61.4 11.4 %copy.43 = bf16[6,64,66,1]{3,1,2,0:T(8,128)(2,1)} copy(bf16[6,64,66,1]{2,1,3,0:T(8,128)(2,1)S(1)} %collective-permute-done.3) | data formatting | bytes 101376 | tf_op jit(solution)/shard_map/ppermute | solution.py:24
  72.8 11.4 %copy.42 = bf16[6,64,66,1]{3,1,2,0:T(8,128)(2,1)} copy(bf16[6,64,66,1]{2,1,3,0:T(8,128)(2,1)S(1)} %collective-permute-done.2) | data formatting | bytes 101376 | tf_op jit(solution)/shard_map/ppermute | solution.py:22
  84.2 22.1 %fusion = f32[6,64,66,130]{3,1,2,0:T(8,128)} fusion(bf16[6,64,66,1]{3,1,2,0:T(8,128)(2,1)} %copy.43, bf16[6,64,1,128]{3,1,2,0:T(8,128)(2,1)S(1)} %collective-permute-done.1, bf16[1,64,64,128]{3,1,2,0:T(8,128)(2,1)S(1)} %get-tuple-element.24, bf16[1,64,64,128]{3,1,2,0:T(8,128)(2,1)S(1)} %get-tuple-element.25, bf16[4,64,64,128]{3,1,2,0:T(8,128)(2,1)} %copy-done.1, ...), kind=kLoop, calls=%fused_computation.17 | loop fusion | flops 52715520 | bytes 19768450 | tf_op jit(solution)/shard_map/convert_element_type | solution.py:165
  106.3 10.0 %fusion.2 = (f32[66,66,130]{2,0,1:T(8,128)}, f32[66,66,130]{2,0,1:T(8,128)S(1)}, f32[66,66,130]{2,0,1:T(8,128)S(1)}, f32[66,66,130]{2,0,1:T(8,128)}) fusion(f32[6,64,66,130]{3,1,2,0:T(8,128)} %fusion), kind=kLoop, calls=%fused_computation.24 | loop fusion | bytes 22239360 | tf_op jit(solution)/shard_map/squeeze | solution.py:62
  116.3 28.8 %fusion.45 = f32[64,64,128]{2,0,1:T(8,128)S(1)} fusion(f32[6,64,66,130]{3,1,2,0:T(8,128)} %fusion, f32[66,66,130]{2,0,1:T(8,128)S(1)} %get-tuple-element.16, f32[66,66,130]{2,0,1:T(8,128)S(1)} %get-tuple-element.15, f32[66,66,130]{2,0,1:T(8,128)} %get-tuple-element.17, bf16[64,64,128]{2,1,0:T(8,128)(2,1)S(1)} %copy-done.10), kind=kLoop, calls=%fused_computation.71 | loop fusion | flops 19922944 | bytes 62652416 | tf_op jit(solution)/shard_map/add | solution.py:71
  147.2 9.4 %convolution_bitcast_fusion = f32[512,64,64]{0,2,1:T(8,128)} fusion(f32[64,64,128]{2,0,1:T(8,128)S(1)} %fusion.139, f32[128,512]{1,0:T(8,128)S(1)} %copy-done), kind=kOutput, calls=%fused_computation.29 | convolution fusion | flops 3221225472 | bytes 10747904 | tf_op jit(solution)/shard_map/lar,rm->mla/dot_general | solution.py:32
  156.6 73.1 %reduce-scatter.2.cloned.1.call-done = f32[128,64,64]{0,2,1:T(8,128)} async-done(((f32[512,64,64]{0,2,1:T(8,128)}), f32[128,64,64]{0,2,1:T(8,128)}) %reduce-scatter.2.cloned.1.call-update) | async-done | bytes 2097168 | tf_op jit(solution)/shard_map/reduce_scatter | solution.py:143
  229.7 5.5 copy.47
  235.2 5.4 reshape.226
  240.7 7.0 %all-to-all-start = ((f32[32,1,16384]{2,1,0:T(1,128)}), f32[32,1,16384]{2,1,0:T(1,128)S(1)}, u32[]{:S(2)}, u32[]{:S(2)}) async-start(f32[32,1,16384]{2,1,0:T(1,128)} %reshape.226), calls=%async_computation.1 | async-start | bytes 4194304 | tf_op jit(solution)/shard_map/all_to_all | solution.py:90
  248.9 26.2 %all-to-all-done = f32[32,1,16384]{2,1,0:T(1,128)S(1)} async-done(((f32[32,1,16384]{2,1,0:T(1,128)}), f32[32,1,16384]{2,1,0:T(1,128)S(1)}, u32[]{:S(2)}, u32[]{:S(2)}) %all-to-all-start) | async-done | bytes 2097184 | tf_op jit(solution)/shard_map/all_to_all | solution.py:90
  277.0 7.4 %reduce = f32[32,16384]{1,0:T(8,128)S(1)} reduce(f32[32,1,16384]{2,1,0:T(1,128)} %copy-done.8, f32[]{:T(128)} %broadcast.258), dimensions={1}, to_apply=%all_to_all.24.reduce_sub_computation | reduce | bytes 4194308 | tf_op jit(solution)/shard_map/all_to_all | solution.py:90
  284.4 3.0 reshape.227
  287.4 6.7 %copy.48 = f32[4,64,32,64]{3,2,1,0:T(8,128)} copy(f32[4,64,32,64]{3,1,0,2:T(8,128)} %bitcast.206) | data formatting | bytes 4194304 | tf_op jit(solution)/shard_map/all_to_all | solution.py:90
  294.1 3.5 reshape.203
  301.5 2.2 fusion.94
  303.7 2.2 fusion.92
  305.8 2.3 add_divide_fusion.1
  308.1 2.6 fusion.133
  310.7 2.2 add_divide_fusion
  321.3 2.3 multiply_bitcast_fusion
  323.5 2.8 copy.66
  326.3 5.3 reshape.228
  331.7 32.7 %all_to_all.33 = f32[32,1,16384]{2,1,0:T(1,128)} all-to-all(f32[32,1,16384]{2,1,0:T(1,128)S(1)} %reshape.228), channel_id=1, replica_groups=mesh['az'=32,'rad'=4] {'az'}, dimensions={0} | all-to-all | bytes 4194304 | tf_op jit(solution)/shard_map/all_to_all | solution.py:135
  364.4 7.4 %reduce.1 = f32[32,16384]{1,0:T(8,128)S(1)} reduce(f32[32,1,16384]{2,1,0:T(1,128)} %all_to_all.33, f32[]{:T(128)} %broadcast.258), dimensions={1}, to_apply=%all_to_all.27.reduce_sub_computation | reduce | bytes 4194308 | tf_op jit(solution)/shard_map/all_to_all | solution.py:135
  371.8 4.2 reshape.229
  376.0 5.3 copy.68
  381.3 5.3 copy.54
  386.6 16.3 %multiply_bitcast_fusion.1 = (f32[64,64,128]{2,0,1:T(8,128)}, f32[1,64,64,128]{3,1,2,0:T(8,128)}, f32[1,64,64,128]{3,1,2,0:T(8,128)}, f32[1,64,64,128]{3,1,2,0:T...) fusion(f32[6,64,66,130]{3,1,2,0:T(8,128)} %fusion), kind=kLoop, calls=%fused_computation.171 | loop fusion | flops 6291456 | bytes 51118080 | tf_op jit(solution)/shard_map/div | solution.py:167
  402.9 17.2 %fusion.73 = f32[1,64,64,128]{3,1,2,0:T(8,128)} fusion(f32[66,66,130]{2,0,1:T(8,128)S(1)} %bitcast.203, f32[6,64,66,130]{3,1,2,0:T(8,128)} %fusion, f32[1,64,64,128]{3,1,2,0:T(8,128)} %get-tuple-element.13, f32[1,64,64,128]{3,1,2,0:T(8,128)} %get-tuple-element.12, f32[1,64,64,128]{3,1,2,0:T(8,128)} %get-tuple-element.11, ...), kind=kLoop, calls=%fused_computation.112 | loop fusion | flops 13631488 | bytes 55312384 | tf_op jit(solution)/shard_map/stack | solution.py:72
  420.1 19.5 %fusion.80 = f32[1,64,64,128]{3,1,2,0:T(8,128)} fusion(f32[66,66,130]{2,0,1:T(8,128)} %get-tuple-element.14, f32[6,64,66,130]{3,1,2,0:T(8,128)} %fusion, f32[1,64,64,128]{3,1,2,0:T(8,128)} %get-tuple-element.13, f32[1,64,64,128]{3,1,2,0:T(8,128)} %get-tuple-element.12, f32[1,64,64,128]{3,1,2,0:T(8,128)} %get-tuple-element.11, ...), kind=kLoop, calls=%fused_computation.124 | loop fusion | flops 13631488 | bytes 55312384 | tf_op jit(solution)/shard_map/stack | solution.py:72
  439.6 18.4 %fusion.87 = f32[1,64,64,128]{3,1,2,0:T(8,128)} fusion(f32[66,66,130]{2,0,1:T(8,128)} %get-tuple-element.14, f32[6,64,66,130]{3,1,2,0:T(8,128)} %fusion, f32[1,64,64,128]{3,1,2,0:T(8,128)} %get-tuple-element.13, f32[1,64,64,128]{3,1,2,0:T(8,128)} %get-tuple-element.12, f32[1,64,64,128]{3,1,2,0:T(8,128)} %get-tuple-element.11, ...), kind=kLoop, calls=%fused_computation.136 | loop fusion | flops 13631488 | bytes 55312384 | tf_op jit(solution)/shard_map/stack | solution.py:72
  458.0 4.5 fusion.1
  462.5 2.2 multiply_reduce_fusion
  464.8 10.2 %fusion.120 = f32[64,64,128]{2,0,1:T(8,128)S(1)} fusion(f32[512,64,64]{0,1,2:T(8,128)} %all-gather.2.cloned.1.call-done, f32[128,512]{1,0:T(8,128)S(1)} %copy-done), kind=kOutput, calls=%fused_computation.181 | convolution fusion | flops 3221225472 | bytes 10747904 | tf_op jit(solution)/shard_map/mla,rm->lar/dot_general | solution.py:32
  475.0 4.0 multiply_reduce_fusion.1
  480.1 64.7 %all-reduce.1 = (f32[]{:T(128)}, f32[]{:T(128)}) all-reduce(f32[]{:T(128)} %fusion.1, f32[]{:T(128)S(6)} %add.397), channel_id=1, replica_groups=mesh['az'=32,'rad'=4] {'az','rad'}, use_global_device_ids=true, to_apply=%region_1.2 | all-reduce | flops 2 | bytes 16 | tf_op jit(solution)/shard_map/psum | solution.py:171
  546.0 4.1 multiply_convert_fusion
  550.8 4.7 copy.55
  (60 shorter events, 21.8 us)
Async XLA Ops:
  6.5 140.7 %copy-start = (f32[128,512]{1,0:T(8,128)S(1)}, f32[128,512]{1,0:T(8,128)}, u32[]{:S(2)}) copy-start(f32[128,512]{1,0:T(8,128)} %param.10) | copy-start | bytes 786436
  6.5 5.1 copy-start.11
  6.5 223.1 %reduce-scatter.2.cloned.1.call-start = ((), (), s32[]{:S(2)}) async-start(), calls=%async_computation.3 | async-start | bytes 10485760 | tf_op jit(solution)/shard_map/reduce_scatter | solution.py:143
  6.5 5.1 copy-start.12
  11.6 2.0 copy-start.1
  13.7 9.5 %collective-permute-start.1 = (bf16[6,64,1,128]{3,1,2,0:T(8,128)(2,1)S(1)}, bf16[6,64,1,128]{3,1,2,0:T(8,128)(2,1)S(1)}, u32[]{:S(2)}, u32[]{:S(2)}) collective-permute-start(bf16[6,64,1,128]{3,1,2,0:T(8,128)(2,1)S(1)} %get-tuple-element.21), channel_id=1, source_target_pairs={{4,0},{8,4},{12,8},{16,12},{20,16},{24,20},{28,24},{32,28},{36,32}... | collective-permute-start | bytes 294920 | tf_op jit(solution)/shard_map/ppermute | solution.py:24
  21.5 7.7 %collective-permute-start = (bf16[6,64,1,128]{3,1,2,0:T(8,128)(2,1)S(1)}, bf16[6,64,1,128]{3,1,2,0:T(8,128)(2,1)S(1)}, u32[]{:S(2)}, u32[]{:S(2)}) collective-permute-start(bf16[6,64,1,128]{3,1,2,0:T(8,128)(2,1)S(1)} %get-tuple-element.20), channel_id=1, source_target_pairs={{0,4},{4,8},{8,12},{12,16},{16,20},{20,24},{24,28},{28,32},{32,36}... | collective-permute-start | bytes 294920 | tf_op jit(solution)/shard_map/ppermute | solution.py:22
  47.9 13.4 %collective-permute-start.3 = (bf16[6,64,66,1]{2,1,3,0:T(8,128)(2,1)S(1)}, bf16[6,64,66,1]{2,1,3,0:T(8,128)(2,1)S(1)}, u32[]{:S(2)}, u32[]{:S(2)}) collective-permute-start(bf16[6,64,66,1]{2,1,3,0:T(8,128)(2,1)S(1)} %copy.41), channel_id=1, source_target_pairs={{1,0},{2,1},{3,2},{0,3},{5,4},{6,5},{7,6},{4,7},{9,8},{10,9},{11,1... | collective-permute-start | bytes 152072 | tf_op jit(solution)/shard_map/ppermute | solution.py:24
  58.6 14.2 %collective-permute-start.2 = (bf16[6,64,66,1]{2,1,3,0:T(8,128)(2,1)S(1)}, bf16[6,64,66,1]{2,1,3,0:T(8,128)(2,1)S(1)}, u32[]{:S(2)}, u32[]{:S(2)}) collective-permute-start(bf16[6,64,66,1]{2,1,3,0:T(8,128)(2,1)S(1)} %copy.40), channel_id=1, source_target_pairs={{0,1},{1,2},{2,3},{3,0},{4,5},{5,6},{6,7},{7,4},{8,9},{9,10},{10,1... | collective-permute-start | bytes 152072 | tf_op jit(solution)/shard_map/ppermute | solution.py:22
  106.3 10.0 %copy-start.10 = (bf16[64,64,128]{2,1,0:T(8,128)(2,1)S(1)}, bf16[64,64,128]{2,1,0:T(8,128)(2,1)}, u32[]{:S(2)}) copy-start(bf16[64,64,128]{2,1,0:T(8,128)(2,1)} %param.7) | copy-start | bytes 3145732
  145.1 2.1 copy-start.2
  240.7 34.5 %all-to-all-start = ((f32[32,1,16384]{2,1,0:T(1,128)}), f32[32,1,16384]{2,1,0:T(1,128)S(1)}, u32[]{:S(2)}, u32[]{:S(2)}) async-start(f32[32,1,16384]{2,1,0:T(1,128)} %reshape.226), calls=%async_computation.1 | async-start | bytes 4194304 | tf_op jit(solution)/shard_map/all_to_all | solution.py:90
  247.6 217.1 %all-gather.2.cloned.1.call-start = ((), (), s32[]{:S(2)}) async-start(), calls=%async_computation.4 | async-start | bytes 10485760 | tf_op jit(solution)/shard_map/all_gather | solution.py:151
  275.1 1.3 copy-start.8
  386.5 16.3 %slice-start = ((s8[4866048]{0:T(1024)(128)(4,1)}), s8[671744]{0:T(1024)(128)(4,1)S(1)}, s32[]{:S(2)}) async-start(s8[4866048]{0:T(1024)(128)(4,1)} %bitcast.202), calls=%async_computation.5 | async-start | bytes 1343488
  386.6 16.3 %slice-start.1 = ((s8[4866048]{0:T(1024)(128)(4,1)}), s8[4194304]{0:T(1024)(128)(4,1)S(1)}, s32[]{:S(2)}) async-start(s8[4866048]{0:T(1024)(128)(4,1)} %bitcast.202), calls=%async_computation.6 | async-start | bytes 8388608
  439.6 18.4 %copy-start.3 = (f32[64,64,128]{2,0,1:T(8,128)S(1)}, f32[64,64,128]{2,0,1:T(8,128)}, u32[]{:S(2)}) copy-start(f32[64,64,128]{2,0,1:T(8,128)} %copy-done.2) | copy-start | bytes 6291460
  439.6 18.4 %copy-start.4 = (f32[1,64,64,128]{3,1,2,0:T(8,128)S(1)}, f32[1,64,64,128]{3,1,2,0:T(8,128)}, u32[]{:S(2)}) copy-start(f32[1,64,64,128]{3,1,2,0:T(8,128)} %fusion.73) | copy-start | bytes 6291460
  458.0 4.5 copy-start.5
  458.0 4.5 copy-start.6
  458.0 4.5 copy-start.7
  546.0 4.2 copy-start.9
Sparse Core Ops, SparseCore 0:
  156.7 72.8 reduce-scatter.1
  386.7 64.0 all-gather.1
where the time goes:
time: 571 us; the launch traced here: 563 us
  other arithmetic  153 us (27%)
  local copies, waits for them, and re-layouts  117 us (20%)
  waiting for transfers between devices  107 us (19%)
  blocking collectives  97.4 us (17%)
  matrix products  51.5 us (9%)
  starting transfers between devices  20 us (4%)
  between operations  16.6 us (3%)
    reduce_scatter x1, waiting for transfers between devices, precondition(): lax.psum_scatter(contract('lar,rm->mla', heights, columns), 'rad', scatte...  73.1 us
    psum x1, blocking collectives, body(): total_rr, total_rz = lax.psum((local_rr, local_rz), ('az', 'rad'))  64.7 us
    another operation x3, other arithmetic, stencil(): return (jnp.stack(parts), diagonal)  55 us
    dot_general x16, matrix products, contract(): jnp.einsum(form, left, right, precision=lax.Precision.HIGHEST, preferred_...  51.5 us
    all_to_all x1, blocking collectives, spectral_solve(): return lax.all_to_all(signal, 'az', split_axis=2, concat_axis=0, tiled=True)  32.7 us
    add x1, other arithmetic, stencil(): source_block + biot_coupling * spread + storage * center[3] + fluid  28.8 us
    all_to_all x1, waiting for transfers between devices, spectral_solve(): lax.all_to_all(coeffs, 'az', split_axis=0, concat_axis=2, tiled=True)  26.2 us
    unnamed x35, local copies, waits for them, and re-layouts  25.1 us
  transfers between devices with their start and end apart: 7, of which 4 were waited for; matrix products, arithmetic and copies ran while one was open for 18% of the time, Pallas kernels for 0%

commit v1 on v0

v1 whole, which is shorter than its diff:
```python
import functools
import math

import jax
import jax.numpy as jnp
import numpy as np
from jax import lax
from jax.experimental import pallas as pl
from jax.experimental.pallas import tpu as pltpu
from jax.sharding import PartitionSpec as P

NH = 64
BA = 64
BR = 128
NRAD = 4
NAZ = 32
LV = NH // NRAD
NM = NRAD * BR
CA = 8
NCH = BA // CA
HB = 4
ROW = 80
PAD = 8

BIOT = 2.0
STORAGE = 1.0

F32 = jnp.float32
BF16 = jnp.bfloat16
WIRE = F32
MESH = pl.DeviceIdType.MESH

ORDER = (3, 5, 0, 1, 2, 4)


def split(x):
    hi = x.astype(BF16)
    lo = (x - hi.astype(F32)).astype(BF16)
    return hi, lo


def cosine_tables():
    l = np.arange(NH, dtype=np.float64)[:, None]
    h = np.arange(NH, dtype=np.float64)[None, :]
    scale = np.where(l == 0, math.sqrt(1.0 / NH), math.sqrt(2.0 / NH))
    table = jnp.asarray(scale * np.cos(math.pi * (h + 0.5) * l / NH), F32)
    out = []
    for c in (table, table.T):
        hi, lo = split(c)
        out.append(jnp.concatenate([hi, lo, hi], axis=1))
    return out


def remote(src, dst, send, recv, device):
    return pltpu.make_async_remote_copy(
        src_ref=src, dst_ref=dst, send_sem=send, recv_sem=recv,
        device_id=device, device_id_type=MESH,
    )


def dot(a, b, dims=((1,), (0,))):
    return lax.dot_general(a, b, (dims, ((), ())), preferred_element_type=F32)


def dot3(xh, xl, bh, bl, dims):
    return dot(xh, bh, dims) + (dot(xl, bh, dims) + dot(xh, bl, dims))


def kernel(
    state, source, shear, perm, basis, eigen, fwd_tab, inv_tab, out,
    xb, ext, qs, ql, qr, pk, ahs, ahr, ah32,
    tmp, mom, fs, fr, coef, ysol, gq, gs, gr, pr,
    bas, bhi, blo, cs, cr, acc, red, redr,
    in_sem, out_sem, hs, hr, as_, ar_, bs, br_, fss, frs, gss, grs, css, crs, rss, rrs,
):
    az = lax.axis_index("az")
    rad = lax.axis_index("rad")
    mate = rad + 1 - 2 * lax.rem(rad, 2)
    across = lax.rem(rad + 2, NRAD)
    az_up = lax.rem(az + 1, NAZ)
    az_dn = lax.rem(az + NAZ - 1, NAZ)
    rad_up = lax.rem(rad + 1, NRAD)
    rad_dn = lax.rem(rad + NRAD - 1, NRAD)
    axx = lax.rem(az, 4)
    azy = az // 4
    x_peers = [(azy * 4 + lax.rem(axx + d, 4), rad) for d in range(1, 4)]
    zy_peers = [(lax.rem(azy + d, 8) * 4 + axx, rad) for d in range(1, 8)]
    rad_peers = [(az, lax.rem(rad + d, NRAD)) for d in range(1, NRAD)]

    def load(f):
        if f < 4:
            src = state.at[f]
        else:
            src = (shear, perm)[f - 4]
        return pltpu.make_async_copy(src, xb.at[f], in_sem.at[f])

    for f in ORDER:
        load(f).start()
    own_basis = pltpu.make_async_copy(basis, bas.at[rad], in_sem.at[7])
    own_basis.start()
    src_load = pltpu.make_async_copy(source, xb.at[6], in_sem.at[6])
    src_load.start()

    barrier = pltpu.get_barrier_semaphore()
    partners = rad_peers + x_peers + zy_peers + [(az_up, rad), (az_dn, rad)]
    for peer in partners:
        pl.semaphore_signal(barrier, inc=1, device_id=peer, device_id_type=MESH)
    pl.semaphore_wait(barrier, len(partners))

    lane = lax.broadcasted_iota(jnp.int32, (BA, BR), 1)
    zero_row = jnp.zeros((ROW, BR), F32)
    halo = []
    for n, f in enumerate(ORDER):
        load(f).wait()
        ext[f, 0] = zero_row
        ext[f, NH + 1] = zero_row

        def stage(h, q, f=f):
            x = xb[f, h].astype(F32)
            ext[f, h + 1, pl.ds(PAD, BA), :] = x
            ah32[0, pl.ds(h, 1), :] = x[0:1]
            ah32[1, pl.ds(h, 1), :] = x[BA - 1 : BA]
            rolled = pltpu.roll(x, 2 * h + 1, 1)
            return jnp.where(lane // 2 == h, rolled, q)

        q = lax.fori_loop(0, NH, stage, jnp.zeros((BA, BR), F32))
        qs[f] = q.astype(BF16)
        ahs[f, 0] = ah32[0].astype(BF16)
        ahs[f, 1] = ah32[1].astype(BF16)
        one = [
            remote(qs.at[f], ql.at[f], hs.at[f, 0], hr.at[f, 0], (az, rad_up)),
            remote(qs.at[f], qr.at[f], hs.at[f, 1], hr.at[f, 1], (az, rad_dn)),
            remote(ahs.at[f, 1], ahr.at[f, 0], as_.at[f, 0], ar_.at[f, 0], (az_up, rad)),
            remote(ahs.at[f, 0], ahr.at[f, 1], as_.at[f, 1], ar_.at[f, 1], (az_dn, rad)),
        ]
        for c in one:
            c.start()
        halo.append((f, one))

    own_basis.wait()
    b_mate = remote(bas.at[rad], bas.at[rad], bs.at[0], br_.at[0], (az, mate))
    b_across = remote(bas.at[rad], bas.at[rad], bs.at[1], br_.at[1], (az, across))
    b_relay = remote(bas.at[across], bas.at[across], bs.at[2], br_.at[2], (az, mate))
    b_mate.start()
    b_across.start()

    even = lax.rem(lane, 2) == 0

    def finish_halo(entry):
        f, one = entry
        for c in one:
            c.wait_recv()
        left = jnp.where(rad > 0, ql[f].astype(F32), 0.0)
        right = jnp.where(rad < NRAD - 1, qr[f].astype(F32), 0.0)
        pk[f] = jnp.where(even, pltpu.roll(right, BR - 1, 1), pltpu.roll(left, 1, 1))
        ah32[0] = ahr[f, 0].astype(F32)
        ah32[1] = ahr[f, 1].astype(F32)

        def place(h, carry):
            ext[f, h + 1, pl.ds(PAD - 1, 1), :] = ah32[0, pl.ds(h, 1), :]
            ext[f, h + 1, pl.ds(PAD + BA, 1), :] = ah32[1, pl.ds(h, 1), :]
            return carry

        lax.fori_loop(0, NH, place, 0)

    for entry in halo[:5]:
        finish_halo(entry)

    lane3 = lax.broadcasted_iota(jnp.int32, (HB, CA, BR), 2)
    first = lane3 == 0
    last = lane3 == BR - 1

    def block(f, h0, c, dh=0, da=0):
        return ext[f, pl.ds(h0 + 1 + dh, HB), pl.ds(PAD + CA * c + da, CA), :]

    def radial_pair(f, h0, c, v):
        tile = pk[f, pl.ds(pl.multiple_of(CA * c, CA), CA), :]
        ends = jnp.stack([pltpu.roll(tile, 127 - 2 * (h0 + i), 1) for i in range(HB)])
        up = jnp.where(last, ends, pltpu.roll(v, BR - 1, 2))
        down = jnp.where(first, ends, pltpu.roll(v, 1, 2))
        return up, down

    def neighbours(f, h0, c):
        v = block(f, h0, c)
        up, down = radial_pair(f, h0, c, v)
        return v, (
            (block(f, h0, c, dh=1), block(f, h0, c, dh=-1)),
            (block(f, h0, c, da=1), block(f, h0, c, da=-1)),
            (up, down),
        )

    src_load.wait()

    def fluid_chunk(c, rr):
        def rows(b, rr):
            h0 = b * HB
            k, ks = neighbours(5, h0, c)
            p, ps = neighbours(3, h0, c)
            total = jnp.zeros_like(p)
            for axis in range(3):
                for side in range(2):
                    total = total + (k + ks[axis][side]) * (p - ps[axis][side])
            u0 = block(0, h0, c)
            up, down = radial_pair(0, h0, c, u0)
            spread = up - down
            spread = spread + (block(1, h0, c, da=1) - block(1, h0, c, da=-1))
            spread = spread + (block(2, h0, c, dh=1) - block(2, h0, c, dh=-1))
            s = xb[6, pl.ds(h0, HB), pl.ds(pl.multiple_of(2 * CA * (c // 2), 2 * CA), 2 * CA), :].astype(F32)
            s = jnp.where(lax.rem(c, 2) == 0, s[:, :CA], s[:, CA:])
            res = s + (0.5 * BIOT) * spread + STORAGE * p + 0.5 * total
            tmp[pl.ds(pl.multiple_of(h0 * CA, CA), HB * CA), :] = res.reshape(HB * CA, BR)
            return rr + jnp.sum(res * res, axis=0)

        rr = lax.fori_loop(0, NH // HB, rows, rr)
        table = fwd_tab[...]
        for pair in range(CA // 2):
            cols = []
            for i in range(2):
                x = tmp[pl.ds(2 * pair + i, NH, stride=CA), :]
                hi, lo = split(x)
                cols.append(jnp.concatenate([hi, hi, lo], axis=0))
            y = dot(table, jnp.concatenate(cols, axis=1))
            for i in range(2):
                for d in range(NRAD):
                    fs[d, c * CA + 2 * pair + i] = y[LV * d : LV * (d + 1), BR * i : BR * (i + 1)].astype(WIRE)
        for d in range(1, NRAD):
            fwd_copy(c, d).start()
        return rr

    def fwd_copy(c, d):
        t = lax.rem(rad + d, NRAD)
        sl = pl.ds(c * CA, CA)
        return remote(fs.at[t, sl], fr.at[rad, sl], fss.at[d, c], frs.at[d, c], (az, t))

    rr = lax.fori_loop(0, NCH, fluid_chunk, jnp.zeros((CA, BR), F32))

    b_across.wait_recv()
    b_relay.start()
    finish_halo(halo[5])

    def moment_chunk(c, carry):
        def rows(b, carry):
            rr, rz = carry
            h0 = b * HB
            g, gs_ = neighbours(4, h0, c)
            face = [[g + gs_[axis][side] for side in range(2)] for axis in range(3)]
            diag2 = (face[0][0] + face[0][1]) + (face[1][0] + face[1][1]) + (face[2][0] + face[2][1])
            p = block(3, h0, c)
            up, down = radial_pair(3, h0, c, p)
            grads = (
                up - down,
                block(3, h0, c, da=1) - block(3, h0, c, da=-1),
                block(3, h0, c, dh=1) - block(3, h0, c, dh=-1),
            )
            inv = 2.0 / diag2
            for f in range(3):
                u, us = neighbours(f, h0, c)
                total = jnp.zeros_like(u)
                for axis in range(3):
                    for side in range(2):
                        total = total + face[axis][side] * (u - us[axis][side])
                res = -(0.5 * total + (0.5 * BIOT) * grads[f])
                step = res * inv
                mom[f, pl.ds(h0, HB), pl.ds(pl.multiple_of(CA * c, CA), CA), :] = step
                rr = rr + jnp.sum(res * res, axis=0)
                rz = rz + jnp.sum(res * step, axis=0)
            return rr, rz

        return lax.fori_loop(0, NH // HB, rows, carry)

    rr, rz = lax.fori_loop(0, NCH, moment_chunk, (rr, jnp.zeros((CA, BR), F32)))
    acc[pl.ds(0, CA), :] = rr

    b_mate.wait_recv()
    b_relay.wait_recv()
    for j in range(NRAD):
        hi, lo = split(bas[j])
        bhi[pl.ds(j * BR, BR), :] = hi
        blo[pl.ds(j * BR, BR), :] = lo

    level = (lax.broadcasted_iota(jnp.int32, (LV, NM), 0) + LV * rad).astype(F32)
    half = jnp.sin(level * (math.pi / (2.0 * NH)))
    sigma = STORAGE + eigen[...] + 4.0 * half * half
    root = jnp.sqrt(sigma * (sigma + 4.0))
    lam = 2.0 / (sigma + 2.0 + root)
    inv_root = 1.0 / root

    def fwd_chunk(c, carry):
        y, w, power = carry
        for d in range(1, NRAD):
            src = lax.rem(rad + NRAD - d, NRAD)
            sl = pl.ds(c * CA, CA)
            remote(fs.at[src, sl], fr.at[src, sl], fss.at[d, c], frs.at[d, c], (az, src)).wait_recv()
        fr[rad, pl.ds(c * CA, CA)] = fs[rad, pl.ds(c * CA, CA)]
        x = jnp.concatenate(
            [fr[j, pl.ds(c * CA, CA)].astype(F32).reshape(CA * LV, BR) for j in range(NRAD)], axis=1
        )
        hi, lo = split(x)
        z = dot3(hi, lo, bhi[...], blo[...], ((1,), (0,)))
        coef[pl.ds(pl.multiple_of(c * CA * LV, CA * LV), CA * LV), :] = z
        for i in range(CA):
            f = z[i * LV : (i + 1) * LV]
            y = lam * y + f
            w = w + power * f
            power = power * lam
        return y, w, power

    zero = jnp.zeros((LV, NM), F32)
    y, w, _ = lax.fori_loop(0, NCH, fwd_chunk, (zero, zero, jnp.ones((LV, NM), F32)))
    cs[0] = y
    cs[1] = w
    c_up = remote(cs.at[0], cr.at[0], css.at[0], crs.at[0], (az_up, rad))
    c_dn = remote(cs.at[1], cr.at[1], css.at[1], crs.at[1], (az_dn, rad))
    c_up.start()
    c_dn.start()
    c_up.wait_recv()

    def sweep_up(a, y):
        rows = pl.ds(pl.multiple_of(a * LV, LV), LV)
        y = lam * y + coef[rows, :]
        ysol[rows, :] = y
        return y

    lax.fori_loop(0, BA, sweep_up, cr[0])
    c_dn.wait_recv()

    def back_copy(c, d):
        t = lax.rem(rad + d, NRAD)
        sl = pl.ds(c * CA, CA)
        return remote(gs.at[t, sl], gr.at[rad, sl], gss.at[d, c], grs.at[d, c], (az, t))

    def back_chunk(n, carry):
        w, fq = carry
        c = NCH - 1 - n

        def cell(i, carry):
            w, fq = carry
            a = CA - 1 - i
            rows = pl.ds(pl.multiple_of((c * CA + a) * LV, LV), LV)
            f = coef[rows, :]
            lw = lam * w
            q = (ysol[rows, :] + lw) * inv_root
            gq[pl.ds(pl.multiple_of(a * LV, LV), LV), :] = q
            return f + lw, fq + f * q

        w, fq = lax.fori_loop(0, CA, cell, (w, fq))
        hi, lo = split(gq[...])
        z = dot3(hi, lo, bhi[...], blo[...], ((1,), (1,)))
        for j in range(NRAD):
            gs[j, pl.ds(c * CA, CA)] = z[:, BR * j : BR * (j + 1)].reshape(CA, LV, BR).astype(WIRE)
        for d in range(1, NRAD):
            back_copy(c, d).start()
        return w, fq

    _, fq = lax.fori_loop(0, NCH, back_chunk, (cr[1], zero))
    part = rz
    for i in range(LV // CA):
        for j in range(NRAD):
            part = part + fq[CA * i : CA * (i + 1), BR * j : BR * (j + 1)]
    acc[pl.ds(CA, CA), :] = part

    total = acc[...]
    base = 0
    for slot, group in enumerate((rad_peers, x_peers, zy_peers)):
        red[slot] = total
        copies = [
            remote(red.at[slot], redr.at[base + i], rss.at[base + i], rrs.at[base + i], peer)
            for i, peer in enumerate(group)
        ]
        for c in copies:
            c.start()
        for i, c in enumerate(copies):
            c.wait_recv()
            total = total + redr[base + i]
        base += len(group)
    alpha = jnp.sum(total[:CA]) / jnp.sum(total[CA:])

    def scale_row(h, carry):
        for f in range(3):
            xb[f, h] = (alpha * mom[f, h]).astype(BF16)
        return carry

    lax.fori_loop(0, NH, scale_row, 0)
    outs = [pltpu.make_async_copy(xb.at[f], out.at[f], out_sem.at[f]) for f in range(3)]
    for o in outs:
        o.start()

    def last_chunk(n, carry):
        c = BA // 16 - 1 - n
        for half_ in range(2):
            cc = 2 * c + 1 - half_
            for d in range(1, NRAD):
                src = lax.rem(rad + NRAD - d, NRAD)
                sl = pl.ds(cc * CA, CA)
                remote(gs.at[src, sl], gr.at[src, sl], gss.at[d, cc], grs.at[d, cc], (az, src)).wait_recv()
        gr[rad, pl.ds(c * 16, 16)] = gs[rad, pl.ds(c * 16, 16)]
        table = inv_tab[...]
        for pair in range(8):
            cols = []
            for i in range(2):
                a = c * 16 + 2 * pair + i
                x = jnp.concatenate([gr[j, a].astype(F32) for j in range(NRAD)], axis=0)
                hi, lo = split(x)
                cols.append(jnp.concatenate([hi, hi, lo], axis=0))
            y = dot(table, jnp.concatenate(cols, axis=1)) * alpha
            for i in range(2):
                pr[pl.ds(2 * pair + i, NH, stride=16), :] = y[:, BR * i : BR * (i + 1)]

        def rows(h, carry):
            xb[3, h, pl.ds(pl.multiple_of(c * 16, 16), 16), :] = pr[pl.ds(pl.multiple_of(h * 16, 16), 16), :].astype(BF16)
            return carry

        lax.fori_loop(0, NH, rows, 0)
        sl = pl.ds(pl.multiple_of(c * 16, 16), 16)
        pltpu.make_async_copy(xb.at[3, :, sl], out.at[3, :, sl], out_sem.at[3 + c]).start()
        return carry

    lax.fori_loop(0, BA // 16, last_chunk, 0)

    for o in outs:
        o.wait()
    for c in range(BA // 16):
        sl = pl.ds(c * 16, 16)
        pltpu.make_async_copy(xb.at[3, :, sl], out.at[3, :, sl], out_sem.at[3 + c]).wait()
    for f, one in halo:
        for c in one:
            c.wait_send()
    for c in (b_mate, b_across, b_relay, c_up, c_dn):
        c.wait_send()
    base = 0
    for slot, group in enumerate((rad_peers, x_peers, zy_peers)):
        for i, peer in enumerate(group):
            remote(red.at[slot], redr.at[base + i], rss.at[base + i], rrs.at[base + i], peer).wait_send()
        base += len(group)

    def drain(c, carry):
        for d in range(1, NRAD):
            fwd_copy(c, d).wait_send()
            back_copy(c, d).wait_send()
        return carry

    lax.fori_loop(0, NCH, drain, 0)


def body(state, source, shear, permeability, radial_basis, radial_eigen):
    fwd_tab, inv_tab = cosine_tables()
    anyspace = pl.BlockSpec(memory_space=pl.ANY)
    vmem = pl.BlockSpec(memory_space=pltpu.VMEM)
    dma = pltpu.SemaphoreType.DMA
    scratch = [
        pltpu.VMEM((7, NH, BA, BR), BF16),
        pltpu.VMEM((6, NH + 2, ROW, BR), F32),
        pltpu.VMEM((6, BA, BR), BF16),
        pltpu.VMEM((6, BA, BR), BF16),
        pltpu.VMEM((6, BA, BR), BF16),
        pltpu.VMEM((6, BA, BR), F32),
        pltpu.VMEM((6, 2, NH, BR), BF16),
        pltpu.VMEM((6, 2, NH, BR), BF16),
        pltpu.VMEM((2, NH, BR), F32),
        pltpu.VMEM((NH * CA, BR), F32),
        pltpu.VMEM((3, NH, BA, BR), F32),
        pltpu.VMEM((NRAD, BA, LV, BR), WIRE),
        pltpu.VMEM((NRAD, BA, LV, BR), WIRE),
        pltpu.VMEM((BA * LV, NM), F32),
        pltpu.VMEM((BA * LV, NM), F32),
        pltpu.VMEM((CA * LV, NM), F32),
        pltpu.VMEM((NRAD, BA, LV, BR), WIRE),
        pltpu.VMEM((NRAD, BA, LV, BR), WIRE),
        pltpu.VMEM((NH * 16, BR), F32),
        pltpu.VMEM((NRAD, BR, NM), F32),
        pltpu.VMEM((NM, NM), BF16),
        pltpu.VMEM((NM, NM), BF16),
        pltpu.VMEM((2, LV, NM), F32),
        pltpu.VMEM((2, LV, NM), F32),
        pltpu.VMEM((2 * CA, BR), F32),
        pltpu.VMEM((3, 2 * CA, BR), F32),
        pltpu.VMEM((13, 2 * CA, BR), F32),
        dma((8,)), dma((8,)),
        dma((6, 2)), dma((6, 2)), dma((6, 2)), dma((6, 2)),
        dma((3,)), dma((3,)),
        dma((NRAD, NCH)), dma((NRAD, NCH)), dma((NRAD, NCH)), dma((NRAD, NCH)),
        dma((2,)), dma((2,)),
        dma((13,)), dma((13,)),
    ]
    return pl.pallas_call(
        kernel,
        out_shape=jax.ShapeDtypeStruct((4, NH, BA, BR), BF16),
        in_specs=[anyspace] * 5 + [vmem] * 3,
        out_specs=anyspace,
        scratch_shapes=scratch,
        compiler_params=pltpu.CompilerParams(
            collective_id=0, has_side_effects=True, vmem_limit_bytes=60 << 20
        ),
        name="residual_step",
    )(state, source, shear, permeability, radial_basis, radial_eigen.reshape(1, NM), fwd_tab, inv_tab)


def solution(mesh):
    placed = (
        P(None, None, "az", "rad"),
        P(None, "az", "rad"),
        P(None, "az", "rad"),
        P(None, "az", "rad"),
        P("rad", None),
        P(),
    )
    return jax.shard_map(
        body, mesh=mesh, in_specs=placed, out_specs=P(None, None, "az", "rad"), check_vma=False
    )
```

time: 571 us -> 128 us (0.22); the launches traced: 563 us -> 127 us
  other arithmetic: 153 us -> 0 us
  Pallas kernels: 0 us -> 122 us
  local copies, waits for them, and re-layouts: 117 us -> 5.16 us
  waiting for transfers between devices: 107 us -> 0 us
  blocking collectives: 97.4 us -> 0 us
  matrix products: 51.5 us -> 0 us
  starting transfers between devices: 20 us -> 0 us
  between operations: 16.6 us -> 0.01 us
    pallas_call x0 -> x1, Pallas kernels: none -> 122 us  [body(): pl.pallas_call(kernel, out_shape=jax.ShapeDtypeStruct((4, NH, BA, BR), BF...]
    reduce_scatter x1 -> x0, waiting for transfers between devices: 73.1 us -> none  [precondition(): lax.psum_scatter(contract('lar,rm->mla', heights, columns), 'rad', scatte...]
    psum x1 -> x0, blocking collectives: 64.7 us -> none  [body(): total_rr, total_rz = lax.psum((local_rr, local_rz), ('az', 'rad'))]
    another operation x3 -> x0, other arithmetic: 55 us -> none  [stencil(): return (jnp.stack(parts), diagonal)]
    dot_general x16 -> x0, matrix products: 51.5 us -> none  [contract(): jnp.einsum(form, left, right, precision=lax.Precision.HIGHEST, preferred_...]
    all_to_all x1 -> x0, blocking collectives: 32.7 us -> none  [spectral_solve(): return lax.all_to_all(signal, 'az', split_axis=2, concat_axis=0, tiled=True)]
    add x3 -> x0, other arithmetic: 29.7 us -> none  [the longest x1 28.8 us: stencil(): source_block + biot_coupling * spread + storage * center[3] + fluid]
    all_to_all x1 -> x0, waiting for transfers between devices: 26.2 us -> none  [spectral_solve(): lax.all_to_all(coeffs, 'az', split_axis=0, concat_axis=2, tiled=True)]
  transfers between devices with their start and end apart: 7 -> 0, of which waited for: 4 -> 0; matrix products, arithmetic and copies ran while one was open for 18% -> 0% of each run, Pallas kernels for 0% -> 0%
where the time goes in v1:
time: 128 us; the launch traced here: 127 us
  Pallas kernels  122 us (95%)
  local copies, waits for them, and re-layouts  5.16 us (4%)
    pallas_call x1, Pallas kernels, body(): pl.pallas_call(kernel, out_shape=jax.ShapeDtypeStruct((4, NH, BA, BR), BF...  122 us
    unnamed x1, local copies, waits for them, and re-layouts  5.16 us

profile of v1, /device:TPU:1, one launch (start us, length us, event | category | flops | bytes accessed | tf_op | source)
XLA Modules:
  0.0 127.1 jit_solution(8707880438665091722)
XLA Ops:
  0.0 121.9 %residual_step.1 = bf16[4,64,64,128]{3,2,1,0:T(8,128)(2,1)} custom-call(bf16[4,64,64,128]{3,2,1,0:T(8,128)(2,1)} %state.1, bf16[64,64,128]{2,1,0:T(8,128)(2,1)} %source.1, bf16[64,64,128]{2,1,0:T(8,128)(2,1)} %shear.1, bf16[64,64,128]{2,1,0:T(8,128)(2,1)} %perm.1, f32[128,512]{1,0:T(8,128)} %basis.1, f32[1,512]{1,0:T(1,128)} %bitcast.1, ...), custom_call_target="tpu_custom_call" | custom-call | tf_op jit(solution)/shard_map/residual_step/pallas_call | solution.py:485
  121.9 5.2 %copy.9 = bf16[4,64,64,128]{3,2,1,0:T(8,128)(2,1)} copy(bf16[4,64,64,128]{3,2,1,0:T(8,128)(2,1)} %residual_step.1) | data formatting | bytes 8388608

commit v2 on v1

--- a/solution.py
+++ b/solution.py
@@ -123,7 +123,7 @@
             rolled = pltpu.roll(x, 2 * h + 1, 1)
             return jnp.where(lane // 2 == h, rolled, q)
 
-        q = lax.fori_loop(0, NH, stage, jnp.zeros((BA, BR), F32))
+        q = lax.fori_loop(0, NH, stage, jnp.zeros((BA, BR), F32), unroll=8)
         qs[f] = q.astype(BF16)
         ahs[f, 0] = ah32[0].astype(BF16)
         ahs[f, 1] = ah32[1].astype(BF16)
@@ -161,7 +161,7 @@
             ext[f, h + 1, pl.ds(PAD + BA, 1), :] = ah32[1, pl.ds(h, 1), :]
             return carry
 
-        lax.fori_loop(0, NH, place, 0)
+        lax.fori_loop(0, NH, place, 0, unroll=8)
 
     for entry in halo[:5]:
         finish_halo(entry)
@@ -211,7 +211,7 @@
             tmp[pl.ds(pl.multiple_of(h0 * CA, CA), HB * CA), :] = res.reshape(HB * CA, BR)
             return rr + jnp.sum(res * res, axis=0)
 
-        rr = lax.fori_loop(0, NH // HB, rows, rr)
+        rr = lax.fori_loop(0, NH // HB, rows, rr, unroll=4)
         table = fwd_tab[...]
         for pair in range(CA // 2):
             cols = []
@@ -266,7 +266,7 @@
                 rz = rz + jnp.sum(res * step, axis=0)
             return rr, rz
 
-        return lax.fori_loop(0, NH // HB, rows, carry)
+        return lax.fori_loop(0, NH // HB, rows, carry, unroll=4)
 
     rr, rz = lax.fori_loop(0, NCH, moment_chunk, (rr, jnp.zeros((CA, BR), F32)))
     acc[pl.ds(0, CA), :] = rr
@@ -321,7 +321,7 @@
         ysol[rows, :] = y
         return y
 
-    lax.fori_loop(0, BA, sweep_up, cr[0])
+    lax.fori_loop(0, BA, sweep_up, cr[0], unroll=8)
     c_dn.wait_recv()
 
     def back_copy(c, d):
@@ -343,7 +343,7 @@
             gq[pl.ds(pl.multiple_of(a * LV, LV), LV), :] = q
             return f + lw, fq + f * q
 
-        w, fq = lax.fori_loop(0, CA, cell, (w, fq))
+        w, fq = lax.fori_loop(0, CA, cell, (w, fq), unroll=True)
         hi, lo = split(gq[...])
         z = dot3(hi, lo, bhi[...], blo[...], ((1,), (1,)))
         for j in range(NRAD):
@@ -380,7 +380,7 @@
             xb[f, h] = (alpha * mom[f, h]).astype(BF16)
         return carry
 
-    lax.fori_loop(0, NH, scale_row, 0)
+    lax.fori_loop(0, NH, scale_row, 0, unroll=4)
     outs = [pltpu.make_async_copy(xb.at[f], out.at[f], out_sem.at[f]) for f in range(3)]
     for o in outs:
         o.start()
@@ -410,7 +410,7 @@
             xb[3, h, pl.ds(pl.multiple_of(c * 16, 16), 16), :] = pr[pl.ds(pl.multiple_of(h * 16, 16), 16), :].astype(BF16)
             return carry
 
-        lax.fori_loop(0, NH, rows, 0)
+        lax.fori_loop(0, NH, rows, 0, unroll=8)
         sl = pl.ds(pl.multiple_of(c * 16, 16), 16)
         pltpu.make_async_copy(xb.at[3, :, sl], out.at[3, :, sl], out_sem.at[3 + c]).start()
         return carry

time: 128 us -> 93.1 us (0.73)
  Pallas kernels: 122 us -> 86.2 us
    pallas_call x1, Pallas kernels: 122 us -> 86.2 us  [body(): pl.pallas_call(kernel, out_shape=jax.ShapeDtypeStruct((4, NH, BA, BR), BF...]
where the time goes in v2:
time: 93.1 us; the launch traced here: 91.3 us
  Pallas kernels  86.2 us (93%)
  local copies, waits for them, and re-layouts  5.16 us (6%)
    pallas_call x1, Pallas kernels, body(): pl.pallas_call(kernel, out_shape=jax.ShapeDtypeStruct((4, NH, BA, BR), BF...  86.2 us
    unnamed x1, local copies, waits for them, and re-layouts  5.16 us

profile of v2, /device:TPU:1, one launch (start us, length us, event | category | flops | bytes accessed | tf_op | source)
XLA Modules:
  0.0 91.3 jit_solution(16472084987546108376)
XLA Ops:
  0.0 86.2 %residual_step.1 = bf16[4,64,64,128]{3,2,1,0:T(8,128)(2,1)} custom-call(bf16[4,64,64,128]{3,2,1,0:T(8,128)(2,1)} %state.1, bf16[64,64,128]{2,1,0:T(8,128)(2,1)} %source.1, bf16[64,64,128]{2,1,0:T(8,128)(2,1)} %shear.1, bf16[64,64,128]{2,1,0:T(8,128)(2,1)} %perm.1, f32[128,512]{1,0:T(8,128)} %basis.1, f32[1,512]{1,0:T(1,128)} %bitcast.1, ...), custom_call_target="tpu_custom_call" | custom-call | tf_op jit(solution)/shard_map/residual_step/pallas_call | solution.py:485
  86.2 5.2 %copy.9 = bf16[4,64,64,128]{3,2,1,0:T(8,128)(2,1)} copy(bf16[4,64,64,128]{3,2,1,0:T(8,128)(2,1)} %residual_step.1) | data formatting | bytes 8388608

commit v3 on v2

--- a/solution.py
+++ b/solution.py
@@ -16,9 +16,9 @@
 NAZ = 32
 LV = NH // NRAD
 NM = NRAD * BR
-CA = 8
+CA = 16
 NCH = BA // CA
-HB = 4
+HB = 2
 ROW = 80
 PAD = 8
 
@@ -27,7 +27,10 @@
 
 F32 = jnp.float32
 BF16 = jnp.bfloat16
-WIRE = F32
+WIRE = BF16
+CODE_SPAN = 152.0
+CODE_BASE = 68.0
+CODE_ZERO = math.exp(-CODE_BASE)
 MESH = pl.DeviceIdType.MESH
 
 ORDER = (3, 5, 0, 1, 2, 4)
@@ -37,6 +40,20 @@
     hi = x.astype(BF16)
     lo = (x - hi.astype(F32)).astype(BF16)
     return hi, lo
+
+
+def encode(x):
+    size = jnp.abs(x)
+    scale = jnp.maximum(jnp.max(size, axis=0), 1e-30).astype(WIRE)
+    rate = CODE_SPAN / scale.astype(F32)
+    y = jnp.exp(size * rate[None] - CODE_BASE) - CODE_ZERO
+    return jnp.where(x < 0, -y, y).astype(WIRE), scale
+
+
+def decode(y, scale):
+    y = y.astype(F32)
+    size = jnp.log(jnp.abs(y) + CODE_ZERO) + CODE_BASE
+    return jnp.where(y < 0, -size, size) * (scale.astype(F32) * (1.0 / CODE_SPAN))
 
 
 def cosine_tables():
@@ -67,9 +84,9 @@
 
 
 def kernel(
-    state, source, shear, perm, basis, eigen, fwd_tab, inv_tab, out,
+    state, source, shear, perm, basis, eigen, fwd_tab, inv_tab, out, alpha_ref,
     xb, ext, qs, ql, qr, pk, ahs, ahr, ah32,
-    tmp, mom, fs, fr, coef, ysol, gq, gs, gr, pr,
+    tmp, lev, mom, fs, fr, xh, xl, coef, ysol, gq, gs, gr, pr,
     bas, bhi, blo, cs, cr, acc, red, redr,
     in_sem, out_sem, hs, hr, as_, ar_, bs, br_, fss, frs, gss, grs, css, crs, rss, rrs,
 ):
@@ -83,9 +100,11 @@
     rad_dn = lax.rem(rad + NRAD - 1, NRAD)
     axx = lax.rem(az, 4)
     azy = az // 4
-    x_peers = [(azy * 4 + lax.rem(axx + d, 4), rad) for d in range(1, 4)]
+    plane_peers = [
+        (azy * 4 + lax.rem(axx + d, 4), lax.rem(rad + e, NRAD))
+        for d in range(4) for e in range(NRAD) if d or e
+    ]
     zy_peers = [(lax.rem(azy + d, 8) * 4 + axx, rad) for d in range(1, 8)]
-    rad_peers = [(az, lax.rem(rad + d, NRAD)) for d in range(1, NRAD)]
 
     def load(f):
         if f < 4:
@@ -102,10 +121,16 @@
     src_load.start()
 
     barrier = pltpu.get_barrier_semaphore()
-    partners = rad_peers + x_peers + zy_peers + [(az_up, rad), (az_dn, rad)]
+    partners = plane_peers + zy_peers + [(az_up, rad), (az_dn, rad)]
     for peer in partners:
         pl.semaphore_signal(barrier, inc=1, device_id=peer, device_id_type=MESH)
     pl.semaphore_wait(barrier, len(partners))
+
+    b_across = remote(basis, bas.at[rad], bs.at[1], br_.at[1], (az, across))
+    b_mate = remote(basis, bas.at[rad], bs.at[0], br_.at[0], (az, mate))
+    b_relay = remote(bas.at[across], bas.at[across], bs.at[2], br_.at[2], (az, mate))
+    b_across.start()
+    b_mate.start()
 
     lane = lax.broadcasted_iota(jnp.int32, (BA, BR), 1)
     zero_row = jnp.zeros((ROW, BR), F32)
@@ -137,13 +162,6 @@
             c.start()
         halo.append((f, one))
 
-    own_basis.wait()
-    b_mate = remote(bas.at[rad], bas.at[rad], bs.at[0], br_.at[0], (az, mate))
-    b_across = remote(bas.at[rad], bas.at[rad], bs.at[1], br_.at[1], (az, across))
-    b_relay = remote(bas.at[across], bas.at[across], bs.at[2], br_.at[2], (az, mate))
-    b_mate.start()
-    b_across.start()
-
     even = lax.rem(lane, 2) == 0
 
     def finish_halo(entry):
@@ -162,6 +180,26 @@
             return carry
 
         lax.fori_loop(0, NH, place, 0, unroll=8)
+
+    def split_basis(j):
+        hi, lo = split(bas[j])
+        rows = pl.ds(pl.multiple_of(j * BR, BR), BR)
+        bhi[rows, :] = hi
+        blo[rows, :] = lo
+
+    own_basis.wait()
+    split_basis(rad)
+    level = (lax.broadcasted_iota(jnp.int32, (LV, NM), 0) + LV * rad).astype(F32)
+    half = jnp.sin(level * (math.pi / (2.0 * NH)))
+    sigma = STORAGE + eigen[...] + 4.0 * half * half
+    root = jnp.sqrt(sigma * (sigma + 4.0))
+    lam = 2.0 / (sigma + 2.0 + root)
+    inv_root = 1.0 / root
+    b_mate.wait_recv()
+    split_basis(mate)
+    b_across.wait_recv()
+    b_relay.start()
+    split_basis(across)
 
     for entry in halo[:5]:
         finish_halo(entry)
@@ -205,8 +243,7 @@
             spread = up - down
             spread = spread + (block(1, h0, c, da=1) - block(1, h0, c, da=-1))
             spread = spread + (block(2, h0, c, dh=1) - block(2, h0, c, dh=-1))
-            s = xb[6, pl.ds(h0, HB), pl.ds(pl.multiple_of(2 * CA * (c // 2), 2 * CA), 2 * CA), :].astype(F32)
-            s = jnp.where(lax.rem(c, 2) == 0, s[:, :CA], s[:, CA:])
+            s = xb[6, pl.ds(h0, HB), pl.ds(pl.multiple_of(CA * c, CA), CA), :].astype(F32)
             res = s + (0.5 * BIOT) * spread + STORAGE * p + 0.5 * total
             tmp[pl.ds(pl.multiple_of(h0 * CA, CA), HB * CA), :] = res.reshape(HB * CA, BR)
             return rr + jnp.sum(res * res, axis=0)
@@ -221,22 +258,24 @@
                 cols.append(jnp.concatenate([hi, hi, lo], axis=0))
             y = dot(table, jnp.concatenate(cols, axis=1))
             for i in range(2):
-                for d in range(NRAD):
-                    fs[d, c * CA + 2 * pair + i] = y[LV * d : LV * (d + 1), BR * i : BR * (i + 1)].astype(WIRE)
+                lev[2 * pair + i] = y[:, BR * i : BR * (i + 1)]
+        for d in range(NRAD):
+            fs[d, c, pl.ds(0, CA)], fs[d, c, CA] = encode(lev[:, pl.ds(LV * d, LV), :])
         for d in range(1, NRAD):
             fwd_copy(c, d).start()
         return rr
 
     def fwd_copy(c, d):
         t = lax.rem(rad + d, NRAD)
-        sl = pl.ds(c * CA, CA)
-        return remote(fs.at[t, sl], fr.at[rad, sl], fss.at[d, c], frs.at[d, c], (az, t))
+        return remote(fs.at[t, c], fr.at[rad, c], fss.at[d, c], frs.at[d, c], (az, t))
 
     rr = lax.fori_loop(0, NCH, fluid_chunk, jnp.zeros((CA, BR), F32))
 
-    b_across.wait_recv()
-    b_relay.start()
     finish_halo(halo[5])
+
+    def mom_copy(c):
+        sl = pl.ds(pl.multiple_of(CA * c, CA), CA)
+        return pltpu.make_async_copy(mom.at[:, :, sl], out.at[pl.ds(0, 3), :, sl], out_sem.at[0, c])
 
     def moment_chunk(c, carry):
         def rows(b, carry):
@@ -266,37 +305,30 @@
                 rz = rz + jnp.sum(res * step, axis=0)
             return rr, rz
 
-        return lax.fori_loop(0, NH // HB, rows, carry, unroll=4)
+        carry = lax.fori_loop(0, NH // HB, rows, carry, unroll=4)
+        mom_copy(c).start()
+        return carry
 
     rr, rz = lax.fori_loop(0, NCH, moment_chunk, (rr, jnp.zeros((CA, BR), F32)))
     acc[pl.ds(0, CA), :] = rr
 
-    b_mate.wait_recv()
     b_relay.wait_recv()
-    for j in range(NRAD):
-        hi, lo = split(bas[j])
-        bhi[pl.ds(j * BR, BR), :] = hi
-        blo[pl.ds(j * BR, BR), :] = lo
-
-    level = (lax.broadcasted_iota(jnp.int32, (LV, NM), 0) + LV * rad).astype(F32)
-    half = jnp.sin(level * (math.pi / (2.0 * NH)))
-    sigma = STORAGE + eigen[...] + 4.0 * half * half
-    root = jnp.sqrt(sigma * (sigma + 4.0))
-    lam = 2.0 / (sigma + 2.0 + root)
-    inv_root = 1.0 / root
+    split_basis(mate + 2 - 4 * (mate // 2))
 
     def fwd_chunk(c, carry):
         y, w, power = carry
         for d in range(1, NRAD):
             src = lax.rem(rad + NRAD - d, NRAD)
-            sl = pl.ds(c * CA, CA)
-            remote(fs.at[src, sl], fr.at[src, sl], fss.at[d, c], frs.at[d, c], (az, src)).wait_recv()
-        fr[rad, pl.ds(c * CA, CA)] = fs[rad, pl.ds(c * CA, CA)]
-        x = jnp.concatenate(
-            [fr[j, pl.ds(c * CA, CA)].astype(F32).reshape(CA * LV, BR) for j in range(NRAD)], axis=1
-        )
-        hi, lo = split(x)
-        z = dot3(hi, lo, bhi[...], blo[...], ((1,), (0,)))
+            remote(fs.at[src, c], fr.at[src, c], fss.at[d, c], frs.at[d, c], (az, src)).wait_recv()
+        fr[rad, c] = fs[rad, c]
+        for j in range(NRAD):
+            scale = fr[j, c, CA]
+            for i in range(0, CA, 4):
+                x = decode(fr[j, c, pl.ds(i, 4)], scale).reshape(4 * LV, BR)
+                hi, lo = split(x)
+                xh[pl.ds(i * LV, 4 * LV), pl.ds(j * BR, BR)] = hi
+                xl[pl.ds(i * LV, 4 * LV), pl.ds(j * BR, BR)] = lo
+        z = dot3(xh[...], xl[...], bhi[...], blo[...], ((1,), (0,)))
         coef[pl.ds(pl.multiple_of(c * CA * LV, CA * LV), CA * LV), :] = z
         for i in range(CA):
             f = z[i * LV : (i + 1) * LV]
@@ -326,8 +358,7 @@
 
     def back_copy(c, d):
         t = lax.rem(rad + d, NRAD)
-        sl = pl.ds(c * CA, CA)
-        return remote(gs.at[t, sl], gr.at[rad, sl], gss.at[d, c], grs.at[d, c], (az, t))
+        return remote(gs.at[t, c], gr.at[rad, c], gss.at[d, c], grs.at[d, c], (az, t))
 
     def back_chunk(n, carry):
         w, fq = carry
@@ -347,96 +378,83 @@
         hi, lo = split(gq[...])
         z = dot3(hi, lo, bhi[...], blo[...], ((1,), (1,)))
         for j in range(NRAD):
-            gs[j, pl.ds(c * CA, CA)] = z[:, BR * j : BR * (j + 1)].reshape(CA, LV, BR).astype(WIRE)
+            gs[j, c, pl.ds(0, CA)], gs[j, c, CA] = encode(z[:, BR * j : BR * (j + 1)].reshape(CA, LV, BR))
         for d in range(1, NRAD):
             back_copy(c, d).start()
         return w, fq
 
     _, fq = lax.fori_loop(0, NCH, back_chunk, (cr[1], zero))
     part = rz
-    for i in range(LV // CA):
-        for j in range(NRAD):
-            part = part + fq[CA * i : CA * (i + 1), BR * j : BR * (j + 1)]
+    for j in range(NRAD):
+        part = part + fq[:, BR * j : BR * (j + 1)]
     acc[pl.ds(CA, CA), :] = part
 
-    total = acc[...]
-    base = 0
-    for slot, group in enumerate((rad_peers, x_peers, zy_peers)):
-        red[slot] = total
-        copies = [
+    def reduce_copies(slot):
+        group, base = ((plane_peers, 0), (zy_peers, len(plane_peers)))[slot]
+        return [
             remote(red.at[slot], redr.at[base + i], rss.at[base + i], rrs.at[base + i], peer)
             for i, peer in enumerate(group)
-        ]
-        for c in copies:
-            c.start()
+        ], base
+
+    def reduce_finish(slot, total):
+        copies, base = reduce_copies(slot)
         for i, c in enumerate(copies):
             c.wait_recv()
             total = total + redr[base + i]
-        base += len(group)
-    alpha = jnp.sum(total[:CA]) / jnp.sum(total[CA:])
-
-    def scale_row(h, carry):
-        for f in range(3):
-            xb[f, h] = (alpha * mom[f, h]).astype(BF16)
-        return carry
-
-    lax.fori_loop(0, NH, scale_row, 0, unroll=4)
-    outs = [pltpu.make_async_copy(xb.at[f], out.at[f], out_sem.at[f]) for f in range(3)]
-    for o in outs:
-        o.start()
+        return total
+
+    def press_copy(c):
+        sl = pl.ds(pl.multiple_of(CA * c, CA), CA)
+        return pltpu.make_async_copy(pr.at[c], out.at[3, :, sl], out_sem.at[1, c])
 
     def last_chunk(n, carry):
-        c = BA // 16 - 1 - n
-        for half_ in range(2):
-            cc = 2 * c + 1 - half_
-            for d in range(1, NRAD):
-                src = lax.rem(rad + NRAD - d, NRAD)
-                sl = pl.ds(cc * CA, CA)
-                remote(gs.at[src, sl], gr.at[src, sl], gss.at[d, cc], grs.at[d, cc], (az, src)).wait_recv()
-        gr[rad, pl.ds(c * 16, 16)] = gs[rad, pl.ds(c * 16, 16)]
+        c = NCH - 1 - n
+        for d in range(1, NRAD):
+            src = lax.rem(rad + NRAD - d, NRAD)
+            remote(gs.at[src, c], gr.at[src, c], gss.at[d, c], grs.at[d, c], (az, src)).wait_recv()
+        gr[rad, c] = gs[rad, c]
         table = inv_tab[...]
-        for pair in range(8):
+        rows = pr.at[c].reshape(NH * CA, BR)
+        for pair in range(CA // 2):
             cols = []
             for i in range(2):
-                a = c * 16 + 2 * pair + i
-                x = jnp.concatenate([gr[j, a].astype(F32) for j in range(NRAD)], axis=0)
+                a = 2 * pair + i
+                x = jnp.concatenate([decode(gr[j, c, a], gr[j, c, CA]) for j in range(NRAD)], axis=0)
                 hi, lo = split(x)
                 cols.append(jnp.concatenate([hi, hi, lo], axis=0))
-            y = dot(table, jnp.concatenate(cols, axis=1)) * alpha
+            y = dot(table, jnp.concatenate(cols, axis=1))
             for i in range(2):
-                pr[pl.ds(2 * pair + i, NH, stride=16), :] = y[:, BR * i : BR * (i + 1)]
-
-        def rows(h, carry):
-            xb[3, h, pl.ds(pl.multiple_of(c * 16, 16), 16), :] = pr[pl.ds(pl.multiple_of(h * 16, 16), 16), :].astype(BF16)
-            return carry
-
-        lax.fori_loop(0, NH, rows, 0, unroll=8)
-        sl = pl.ds(pl.multiple_of(c * 16, 16), 16)
-        pltpu.make_async_copy(xb.at[3, :, sl], out.at[3, :, sl], out_sem.at[3 + c]).start()
+                rows[pl.ds(2 * pair + i, NH, stride=CA), :] = y[:, BR * i : BR * (i + 1)]
+        press_copy(c).start()
         return carry
 
-    lax.fori_loop(0, BA // 16, last_chunk, 0)
-
-    for o in outs:
-        o.wait()
-    for c in range(BA // 16):
-        sl = pl.ds(c * 16, 16)
-        pltpu.make_async_copy(xb.at[3, :, sl], out.at[3, :, sl], out_sem.at[3 + c]).wait()
+    red[0] = acc[...]
+    for c in reduce_copies(0)[0]:
+        c.start()
+    last_chunk(0, 0)
+    total = reduce_finish(0, acc[...])
+    red[1] = total
+    for c in reduce_copies(1)[0]:
+        c.start()
+    lax.fori_loop(1, NCH, last_chunk, 0)
+    total = reduce_finish(1, total)
+    alpha_ref[0, 0] = jnp.sum(total[:CA]) / jnp.sum(total[CA:])
+
     for f, one in halo:
         for c in one:
             c.wait_send()
     for c in (b_mate, b_across, b_relay, c_up, c_dn):
         c.wait_send()
-    base = 0
-    for slot, group in enumerate((rad_peers, x_peers, zy_peers)):
-        for i, peer in enumerate(group):
-            remote(red.at[slot], redr.at[base + i], rss.at[base + i], rrs.at[base + i], peer).wait_send()
-        base += len(group)
+    for slot in range(2):
+        for c in reduce_copies(slot)[0]:
+            c.wait_send()
 
     def drain(c, carry):
         for d in range(1, NRAD):
             fwd_copy(c, d).wait_send()
             back_copy(c, d).wait_send()
+        mom_copy(c).wait()
+        press_copy(c).wait()
         return carry
 
     lax.fori_loop(0, NCH, drain, 0)
@@ -458,41 +476,45 @@
         pltpu.VMEM((6, 2, NH, BR), BF16),
         pltpu.VMEM((2, NH, BR), F32),
         pltpu.VMEM((NH * CA, BR), F32),
+        pltpu.VMEM((CA, NH, BR), F32),
         pltpu.VMEM((3, NH, BA, BR), F32),
-        pltpu.VMEM((NRAD, BA, LV, BR), WIRE),
-        pltpu.VMEM((NRAD, BA, LV, BR), WIRE),
+        pltpu.VMEM((NRAD, NCH, CA + 1, LV, BR), WIRE),
+        pltpu.VMEM((NRAD, NCH, CA + 1, LV, BR), WIRE),
+        pltpu.VMEM((CA * LV, NM), BF16),
+        pltpu.VMEM((CA * LV, NM), BF16),
         pltpu.VMEM((BA * LV, NM), F32),
         pltpu.VMEM((BA * LV, NM), F32),
         pltpu.VMEM((CA * LV, NM), F32),
-        pltpu.VMEM((NRAD, BA, LV, BR), WIRE),
-        pltpu.VMEM((NRAD, BA, LV, BR), WIRE),
-        pltpu.VMEM((NH * 16, BR), F32),
+        pltpu.VMEM((NRAD, NCH, CA + 1, LV, BR), WIRE),
+        pltpu.VMEM((NRAD, NCH, CA + 1, LV, BR), WIRE),
+        pltpu.VMEM((NCH, NH, CA, BR), F32),
         pltpu.VMEM((NRAD, BR, NM), F32),
         pltpu.VMEM((NM, NM), BF16),
         pltpu.VMEM((NM, NM), BF16),
         pltpu.VMEM((2, LV, NM), F32),
         pltpu.VMEM((2, LV, NM), F32),
         pltpu.VMEM((2 * CA, BR), F32),
-        pltpu.VMEM((3, 2 * CA, BR), F32),
-        pltpu.VMEM((13, 2 * CA, BR), F32),
-        dma((8,)), dma((8,)),
+        pltpu.VMEM((2, 2 * CA, BR), F32),
+        pltpu.VMEM((22, 2 * CA, BR), F32),
+        dma((8,)), dma((2, NCH)),
         dma((6, 2)), dma((6, 2)), dma((6, 2)), dma((6, 2)),
         dma((3,)), dma((3,)),
         dma((NRAD, NCH)), dma((NRAD, NCH)), dma((NRAD, NCH)), dma((NRAD, NCH)),
         dma((2,)), dma((2,)),
-        dma((13,)), dma((13,)),
+        dma((22,)), dma((22,)),
     ]
-    return pl.pallas_call(
+    step, alpha = pl.pallas_call(
         kernel,
-        out_shape=jax.ShapeDtypeStruct((4, NH, BA, BR), BF16),
+        out_shape=(jax.ShapeDtypeStruct((4, NH, BA, BR), F32), jax.ShapeDtypeStruct((1, 1), F32)),
         in_specs=[anyspace] * 5 + [vmem] * 3,
-        out_specs=anyspace,
+        out_specs=(anyspace, pl.BlockSpec(memory_space=pltpu.SMEM)),
         scratch_shapes=scratch,
         compiler_params=pltpu.CompilerParams(
             collective_id=0, has_side_effects=True, vmem_limit_bytes=60 << 20
         ),
         name="residual_step",
     )(state, source, shear, permeability, radial_basis, radial_eigen.reshape(1, NM), fwd_tab, inv_tab)
+    return (alpha[0, 0] * step).astype(BF16)
 
 
 def solution(mesh):

time: 93.1 us -> 82 us (0.88); the launches traced: 91.3 us -> 81.8 us
  Pallas kernels: 86.2 us -> 74.6 us
  other arithmetic: 0 us -> 7.2 us
  local copies, waits for them, and re-layouts: 5.16 us -> 0 us
    pallas_call x1, Pallas kernels: 86.2 us -> 74.6 us  [body(): pl.pallas_call(kernel, out_shape=(jax.ShapeDtypeStruct((4, NH, BA, BR), F...]
    convert_element_type x0 -> x1, other arithmetic: none -> 7.2 us  [body(): return (alpha[0, 0] * step).astype(BF16)]
    unnamed x1 -> x0, local copies, waits for them, and re-layouts: 5.16 us -> none
where the time goes in v3:
time: 82 us; the launch traced here: 81.8 us
  Pallas kernels  74.6 us (91%)
  other arithmetic  7.2 us (9%)
    pallas_call x1, Pallas kernels, body(): pl.pallas_call(kernel, out_shape=(jax.ShapeDtypeStruct((4, NH, BA, BR), F...  74.6 us
    convert_element_type x1, other arithmetic, body(): return (alpha[0, 0] * step).astype(BF16)  7.2 us

profile of v3, /device:TPU:1, one launch (start us, length us, event | category | flops | bytes accessed | tf_op | source)
XLA Modules:
  0.0 81.8 jit_solution(283233521348635706)
XLA Ops:
  0.0 74.6 %residual_step.1 = (f32[4,64,64,128]{3,2,1,0:T(8,128)}, f32[1,1]{1,0:T(1,128)}) custom-call(bf16[4,64,64,128]{3,2,1,0:T(8,128)(2,1)} %state.1, bf16[64,64,128]{2,1,0:T(8,128)(2,1)} %source.1, bf16[64,64,128]{2,1,0:T(8,128)(2,1)} %shear.1, bf16[64,64,128]{2,1,0:T(8,128)(2,1)} %perm.1, f32[128,512]{1,0:T(8,128)} %basis.1, f32[1,512]{1,0:T(1,128)} %bitcast.2, ...), custom_call_target="tpu_custom_call" | custom-call | tf_op jit(solution)/shard_map/residual_step/pallas_call | solution.py:506
  74.6 7.2 %multiply_convert_fusion = bf16[4,64,64,128]{3,2,1,0:T(8,128)(2,1)} fusion(f32[4,64,64,128]{3,2,1,0:T(8,128)} %get-tuple-element.8, f32[]{:T(128)} %bitcast.1), kind=kLoop, calls=%fused_computation | loop fusion | flops 4194304 | bytes 12582916 | tf_op jit(solution)/shard_map/convert_element_type | solution.py:517

commit v4 on v3

--- a/solution.py
+++ b/solution.py
@@ -21,6 +21,7 @@
 HB = 2
 ROW = 80
 PAD = 8
+EARLY = 2
 
 BIOT = 2.0
 STORAGE = 1.0
@@ -86,9 +87,9 @@
 def kernel(
     state, source, shear, perm, basis, eigen, fwd_tab, inv_tab, out, alpha_ref,
     xb, ext, qs, ql, qr, pk, ahs, ahr, ah32,
-    tmp, lev, mom, fs, fr, xh, xl, coef, ysol, gq, gs, gr, pr,
+    tmp, lev, fs, fr, xh, xl, coef, ysol, gq, gs, gr,
     bas, bhi, blo, cs, cr, acc, red, redr,
-    in_sem, out_sem, hs, hr, as_, ar_, bs, br_, fss, frs, gss, grs, css, crs, rss, rrs,
+    in_sem, hs, hr, as_, ar_, bs, br_, fss, frs, gss, grs, css, crs, rss, rrs,
 ):
     az = lax.axis_index("az")
     rad = lax.axis_index("rad")
@@ -100,11 +101,14 @@
     rad_dn = lax.rem(rad + NRAD - 1, NRAD)
     axx = lax.rem(az, 4)
     azy = az // 4
-    plane_peers = [
-        (azy * 4 + lax.rem(axx + d, 4), lax.rem(rad + e, NRAD))
-        for d in range(4) for e in range(NRAD) if d or e
+    near_peers = [
+        ((azy // 2) * 8 + lax.rem(azy + d, 2) * 4 + axx, lax.rem(rad + e, NRAD))
+        for d in range(2) for e in range(NRAD) if d or e
     ]
-    zy_peers = [(lax.rem(azy + d, 8) * 4 + axx, rad) for d in range(1, 8)]
+    far_peers = [
+        ((lax.rem(azy // 2 + d, 4) * 2 + lax.rem(azy, 2)) * 4 + lax.rem(axx + e, 4), rad)
+        for d in range(4) for e in range(4) if d or e
+    ]
 
     def load(f):
         if f < 4:
@@ -121,21 +125,15 @@
     src_load.start()
 
     barrier = pltpu.get_barrier_semaphore()
-    partners = plane_peers + zy_peers + [(az_up, rad), (az_dn, rad)]
+    partners = near_peers + far_peers + [(az_up, rad), (az_dn, rad)]
     for peer in partners:
         pl.semaphore_signal(barrier, inc=1, device_id=peer, device_id_type=MESH)
     pl.semaphore_wait(barrier, len(partners))
 
-    b_across = remote(basis, bas.at[rad], bs.at[1], br_.at[1], (az, across))
-    b_mate = remote(basis, bas.at[rad], bs.at[0], br_.at[0], (az, mate))
-    b_relay = remote(bas.at[across], bas.at[across], bs.at[2], br_.at[2], (az, mate))
-    b_across.start()
-    b_mate.start()
-
     lane = lax.broadcasted_iota(jnp.int32, (BA, BR), 1)
     zero_row = jnp.zeros((ROW, BR), F32)
-    halo = []
-    for n, f in enumerate(ORDER):
+    halo = {}
+    def stage_field(f):
         load(f).wait()
         ext[f, 0] = zero_row
         ext[f, NH + 1] = zero_row
@@ -160,13 +158,21 @@
         ]
         for c in one:
             c.start()
-        halo.append((f, one))
+        halo[f] = one
+
+    for f in ORDER[:5]:
+        stage_field(f)
+
+    b_across = remote(basis, bas.at[rad], bs.at[1], br_.at[1], (az, across))
+    b_mate = remote(basis, bas.at[rad], bs.at[0], br_.at[0], (az, mate))
+    b_relay = remote(bas.at[across], bas.at[across], bs.at[2], br_.at[2], (az, mate))
+    b_across.start()
+    b_mate.start()
 
     even = lax.rem(lane, 2) == 0
 
-    def finish_halo(entry):
-        f, one = entry
-        for c in one:
+    def finish_halo(f):
+        for c in halo[f]:
             c.wait_recv()
         left = jnp.where(rad > 0, ql[f].astype(F32), 0.0)
         right = jnp.where(rad < NRAD - 1, qr[f].astype(F32), 0.0)
@@ -195,14 +201,8 @@
     root = jnp.sqrt(sigma * (sigma + 4.0))
     lam = 2.0 / (sigma + 2.0 + root)
     inv_root = 1.0 / root
-    b_mate.wait_recv()
-    split_basis(mate)
-    b_across.wait_recv()
-    b_relay.start()
-    split_basis(across)
-
-    for entry in halo[:5]:
-        finish_halo(entry)
+    for f in ORDER[:4]:
+        finish_halo(f)
 
     lane3 = lax.broadcasted_iota(jnp.int32, (HB, CA, BR), 2)
     first = lane3 == 0
@@ -269,13 +269,17 @@
         t = lax.rem(rad + d, NRAD)
         return remote(fs.at[t, c], fr.at[rad, c], fss.at[d, c], frs.at[d, c], (az, t))
 
-    rr = lax.fori_loop(0, NCH, fluid_chunk, jnp.zeros((CA, BR), F32))
-
-    finish_halo(halo[5])
-
-    def mom_copy(c):
-        sl = pl.ds(pl.multiple_of(CA * c, CA), CA)
-        return pltpu.make_async_copy(mom.at[:, :, sl], out.at[pl.ds(0, 3), :, sl], out_sem.at[0, c])
+    rr = lax.fori_loop(0, NCH // 2, fluid_chunk, jnp.zeros((CA, BR), F32))
+    stage_field(ORDER[5])
+    b_mate.wait_recv()
+    split_basis(mate)
+    b_across.wait_recv()
+    b_relay.start()
+    split_basis(across)
+    rr = lax.fori_loop(NCH // 2, NCH, fluid_chunk, rr)
+
+    for f in ORDER[4:]:
+        finish_halo(f)
 
     def moment_chunk(c, carry):
         def rows(b, carry):
@@ -291,26 +295,24 @@
                 block(3, h0, c, da=1) - block(3, h0, c, da=-1),
                 block(3, h0, c, dh=1) - block(3, h0, c, dh=-1),
             )
-            inv = 2.0 / diag2
+            inv = 1.0 / diag2
+            square = jnp.zeros_like(p)
             for f in range(3):
                 u, us = neighbours(f, h0, c)
-                total = jnp.zeros_like(u)
+                res = -BIOT * grads[f] - diag2 * u
                 for axis in range(3):
                     for side in range(2):
-                        total = total + face[axis][side] * (u - us[axis][side])
-                res = -(0.5 * total + (0.5 * BIOT) * grads[f])
+                        res = res + face[axis][side] * us[axis][side]
                 step = res * inv
-                mom[f, pl.ds(h0, HB), pl.ds(pl.multiple_of(CA * c, CA), CA), :] = step
-                rr = rr + jnp.sum(res * res, axis=0)
-                rz = rz + jnp.sum(res * step, axis=0)
-            return rr, rz
-
-        carry = lax.fori_loop(0, NH // HB, rows, carry, unroll=4)
-        mom_copy(c).start()
-        return carry
-
-    rr, rz = lax.fori_loop(0, NCH, moment_chunk, (rr, jnp.zeros((CA, BR), F32)))
-    acc[pl.ds(0, CA), :] = rr
+                for i in range(HB):
+                    out[pl.ds(pl.multiple_of((f * NH + h0 + i) * BA + CA * c, CA), CA), :] = step[i]
+                square = square + res * res
+            return rr + jnp.sum(square, axis=0), rz + jnp.sum(square * inv, axis=0)
+
+        return lax.fori_loop(0, NH // HB, rows, carry, unroll=4)
+
+    quad = jnp.zeros((CA, BR), F32)
+    quad = lax.fori_loop(0, EARLY, moment_chunk, (quad, quad))
 
     b_relay.wait_recv()
     split_basis(mate + 2 - 4 * (mate // 2))
@@ -345,68 +347,69 @@
     c_dn = remote(cs.at[1], cr.at[1], css.at[1], crs.at[1], (az_dn, rad))
     c_up.start()
     c_dn.start()
+    quad = lax.fori_loop(EARLY, NCH, moment_chunk, quad)
+    acc[pl.ds(0, CA), :] = rr + 0.25 * quad[0]
     c_up.wait_recv()
 
-    def sweep_up(a, y):
+    def sweep_up(a, carry):
+        y, yy = carry
         rows = pl.ds(pl.multiple_of(a * LV, LV), LV)
         y = lam * y + coef[rows, :]
         ysol[rows, :] = y
-        return y
-
-    lax.fori_loop(0, BA, sweep_up, cr[0], unroll=8)
+        return y, yy + y * y
+
+    _, yy = lax.fori_loop(0, BA, sweep_up, (cr[0], zero), unroll=8)
+    yy = lam * yy
+    part = 0.5 * quad[1]
+    for j in range(NRAD):
+        part = part + yy[:, BR * j : BR * (j + 1)]
+    acc[pl.ds(CA, CA), :] = part
+
+    def reduce_copies(slot):
+        group, base = ((near_peers, 0), (far_peers, len(near_peers)))[slot]
+        return [
+            remote(red.at[slot], redr.at[base + i], rss.at[base + i], rrs.at[base + i], peer)
+            for i, peer in enumerate(group)
+        ], base
+
+    def reduce_finish(slot, total):
+        copies, base = reduce_copies(slot)
+        for i, c in enumerate(copies):
+            c.wait_recv()
+            total = total + redr[base + i]
+        return total
+
+    red[0] = acc[...]
+    for c in reduce_copies(0)[0]:
+        c.start()
     c_dn.wait_recv()
 
     def back_copy(c, d):
         t = lax.rem(rad + d, NRAD)
         return remote(gs.at[t, c], gr.at[rad, c], gss.at[d, c], grs.at[d, c], (az, t))
 
-    def back_chunk(n, carry):
-        w, fq = carry
+    def back_chunk(n, w):
         c = NCH - 1 - n
 
-        def cell(i, carry):
-            w, fq = carry
+        def cell(i, w):
             a = CA - 1 - i
             rows = pl.ds(pl.multiple_of((c * CA + a) * LV, LV), LV)
             f = coef[rows, :]
             lw = lam * w
             q = (ysol[rows, :] + lw) * inv_root
             gq[pl.ds(pl.multiple_of(a * LV, LV), LV), :] = q
-            return f + lw, fq + f * q
-
-        w, fq = lax.fori_loop(0, CA, cell, (w, fq), unroll=True)
+            return f + lw
+
+        w = lax.fori_loop(0, CA, cell, w, unroll=True)
         hi, lo = split(gq[...])
         z = dot3(hi, lo, bhi[...], blo[...], ((1,), (1,)))
         for j in range(NRAD):
             gs[j, c, pl.ds(0, CA)], gs[j, c, CA] = encode(z[:, BR * j : BR * (j + 1)].reshape(CA, LV, BR))
         for d in range(1, NRAD):
             back_copy(c, d).start()
-        return w, fq
-
-    _, fq = lax.fori_loop(0, NCH, back_chunk, (cr[1], zero))
-    part = rz
-    for j in range(NRAD):
-        part = part + fq[:, BR * j : BR * (j + 1)]
-    acc[pl.ds(CA, CA), :] = part
-
-    def reduce_copies(slot):
-        group, base = ((plane_peers, 0), (zy_peers, len(plane_peers)))[slot]
-        return [
-            remote(red.at[slot], redr.at[base + i], rss.at[base + i], rrs.at[base + i], peer)
-            for i, peer in enumerate(group)
-        ], base
-
-    def reduce_finish(slot, total):
-        copies, base = reduce_copies(slot)
-        for i, c in enumerate(copies):
-            c.wait_recv()
-            total = total + redr[base + i]
-        return total
-
-    def press_copy(c):
-        sl = pl.ds(pl.multiple_of(CA * c, CA), CA)
-        return pltpu.make_async_copy(pr.at[c], out.at[3, :, sl], out_sem.at[1, c])
-
+        return w
+
+    lax.fori_loop(0, NCH, back_chunk, cr[1])
     def last_chunk(n, carry):
         c = NCH - 1 - n
         for d in range(1, NRAD):
@@ -414,7 +417,6 @@
             remote(gs.at[src, c], gr.at[src, c], gss.at[d, c], grs.at[d, c], (az, src)).wait_recv()
         gr[rad, c] = gs[rad, c]
         table = inv_tab[...]
-        rows = pr.at[c].reshape(NH * CA, BR)
         for pair in range(CA // 2):
             cols = []
             for i in range(2):
@@ -424,23 +426,18 @@
                 cols.append(jnp.concatenate([hi, hi, lo], axis=0))
             y = dot(table, jnp.concatenate(cols, axis=1))
             for i in range(2):
-                rows[pl.ds(2 * pair + i, NH, stride=CA), :] = y[:, BR * i : BR * (i + 1)]
-        press_copy(c).start()
+                out[pl.ds(3 * NH * BA + c * CA + 2 * pair + i, NH, stride=BA), :] = y[:, BR * i : BR * (i + 1)]
         return carry
 
-    red[0] = acc[...]
-    for c in reduce_copies(0)[0]:
-        c.start()
-    last_chunk(0, 0)
     total = reduce_finish(0, acc[...])
     red[1] = total
     for c in reduce_copies(1)[0]:
         c.start()
-    lax.fori_loop(1, NCH, last_chunk, 0)
+    lax.fori_loop(0, NCH, last_chunk, 0)
     total = reduce_finish(1, total)
     alpha_ref[0, 0] = jnp.sum(total[:CA]) / jnp.sum(total[CA:])
 
-    for f, one in halo:
+    for one in halo.values():
         for c in one:
             c.wait_send()
     for c in (b_mate, b_across, b_relay, c_up, c_dn):
@@ -453,8 +450,6 @@
         for d in range(1, NRAD):
             fwd_copy(c, d).wait_send()
             back_copy(c, d).wait_send()
-        mom_copy(c).wait()
-        press_copy(c).wait()
         return carry
 
     lax.fori_loop(0, NCH, drain, 0)
@@ -462,7 +457,7 @@
 
 def body(state, source, shear, permeability, radial_basis, radial_eigen):
     fwd_tab, inv_tab = cosine_tables()
-    anyspace = pl.BlockSpec(memory_space=pl.ANY)
+    anyspace = pl.BlockSpec(memory_space=pltpu.HBM)
     vmem = pl.BlockSpec(memory_space=pltpu.VMEM)
     dma = pltpu.SemaphoreType.DMA
     scratch = [
@@ -477,7 +472,6 @@
         pltpu.VMEM((2, NH, BR), F32),
         pltpu.VMEM((NH * CA, BR), F32),
         pltpu.VMEM((CA, NH, BR), F32),
-        pltpu.VMEM((3, NH, BA, BR), F32),
         pltpu.VMEM((NRAD, NCH, CA + 1, LV, BR), WIRE),
         pltpu.VMEM((NRAD, NCH, CA + 1, LV, BR), WIRE),
         pltpu.VMEM((CA * LV, NM), BF16),
@@ -487,7 +481,6 @@
         pltpu.VMEM((CA * LV, NM), F32),
         pltpu.VMEM((NRAD, NCH, CA + 1, LV, BR), WIRE),
         pltpu.VMEM((NRAD, NCH, CA + 1, LV, BR), WIRE),
-        pltpu.VMEM((NCH, NH, CA, BR), F32),
         pltpu.VMEM((NRAD, BR, NM), F32),
         pltpu.VMEM((NM, NM), BF16),
         pltpu.VMEM((NM, NM), BF16),
@@ -496,7 +489,7 @@
         pltpu.VMEM((2 * CA, BR), F32),
         pltpu.VMEM((2, 2 * CA, BR), F32),
         pltpu.VMEM((22, 2 * CA, BR), F32),
-        dma((8,)), dma((2, NCH)),
+        dma((8,)),
         dma((6, 2)), dma((6, 2)), dma((6, 2)), dma((6, 2)),
         dma((3,)), dma((3,)),
         dma((NRAD, NCH)), dma((NRAD, NCH)), dma((NRAD, NCH)), dma((NRAD, NCH)),
@@ -505,16 +498,16 @@
     ]
     step, alpha = pl.pallas_call(
         kernel,
-        out_shape=(jax.ShapeDtypeStruct((4, NH, BA, BR), F32), jax.ShapeDtypeStruct((1, 1), F32)),
+        out_shape=(pltpu.VMEM((4 * NH * BA, BR), F32), jax.ShapeDtypeStruct((1, 1), F32)),
         in_specs=[anyspace] * 5 + [vmem] * 3,
-        out_specs=(anyspace, pl.BlockSpec(memory_space=pltpu.SMEM)),
+        out_specs=(vmem, pl.BlockSpec(memory_space=pltpu.SMEM)),
         scratch_shapes=scratch,
         compiler_params=pltpu.CompilerParams(
-            collective_id=0, has_side_effects=True, vmem_limit_bytes=60 << 20
+            collective_id=0, has_side_effects=True, vmem_limit_bytes=52 << 20
         ),
         name="residual_step",
     )(state, source, shear, permeability, radial_basis, radial_eigen.reshape(1, NM), fwd_tab, inv_tab)
-    return (alpha[0, 0] * step).astype(BF16)
+    return (alpha[0, 0] * step).astype(BF16).reshape(4, NH, BA, BR)
 
 
 def solution(mesh):

time: 82 us -> 67.6 us (0.82)
  Pallas kernels: 74.6 us -> 64.6 us
  other arithmetic: 7.2 us -> 2.81 us
    pallas_call x1, Pallas kernels: 74.6 us -> 64.6 us  [body(): pl.pallas_call(kernel, out_shape=(pltpu.VMEM((4 * NH * BA, BR), F32), jax...]
    convert_element_type x1, other arithmetic: 7.2 us -> 2.81 us  [body(): return (alpha[0, 0] * step).astype(BF16).reshape(4, NH, BA, BR)]
where the time goes in v4:
time: 67.6 us; the launch traced here: 67.4 us
  Pallas kernels  64.6 us (96%)
  other arithmetic  2.81 us (4%)
    pallas_call x1, Pallas kernels, body(): pl.pallas_call(kernel, out_shape=(pltpu.VMEM((4 * NH * BA, BR), F32), jax...  64.6 us
    convert_element_type x1, other arithmetic, body(): return (alpha[0, 0] * step).astype(BF16).reshape(4, NH, BA, BR)  2.81 us

profile of v4, /device:TPU:1, one launch (start us, length us, event | category | flops | bytes accessed | tf_op | source)
XLA Modules:
  0.0 67.4 jit_solution(4872514306581332189)
XLA Ops:
  0.0 64.6 %residual_step.1 = (f32[16384,128]{1,0:T(8,128)S(1)}, f32[1,1]{1,0:T(1,128)}) custom-call(bf16[4,64,64,128]{3,2,1,0:T(8,128)(2,1)} %state.1, bf16[64,64,128]{2,1,0:T(8,128)(2,1)} %source.1, bf16[64,64,128]{2,1,0:T(8,128)(2,1)} %shear.1, bf16[64,64,128]{2,1,0:T(8,128)(2,1)} %perm.1, f32[128,512]{1,0:T(8,128)} %basis.1, f32[1,512]{1,0:T(1,128)} %bitcast.3, ...), custom_call_target="tpu_custom_call" | custom-call | tf_op jit(solution)/shard_map/residual_step/pallas_call | solution.py:499
  64.6 2.8 %multiply_convert_fusion = bf16[16384,128]{1,0:T(8,128)(2,1)} fusion(f32[16384,128]{1,0:T(8,128)S(1)} %get-tuple-element.8, f32[]{:T(128)} %bitcast.1), kind=kLoop, calls=%fused_computation | loop fusion | flops 4194304 | bytes 12582916 | tf_op jit(solution)/shard_map/convert_element_type | solution.py:510

commit v5 on v4

--- a/solution.py
+++ b/solution.py
@@ -87,8 +87,8 @@
 def kernel(
     state, source, shear, perm, basis, eigen, fwd_tab, inv_tab, out, alpha_ref,
     xb, ext, qs, ql, qr, pk, ahs, ahr, ah32,
-    tmp, lev, fs, fr, xh, xl, coef, ysol, gq, gs, gr,
-    bas, bhi, blo, cs, cr, acc, red, redr,
+    tmp, cor, lev, fs, fr, xh, xl, coef, ysol, gq, gs, gr,
+    own, code, bas, bhi, blo, cs, cr, acc, red, redr,
     in_sem, hs, hr, as_, ar_, bs, br_, fss, frs, gss, grs, css, crs, rss, rrs,
 ):
     az = lax.axis_index("az")
@@ -117,10 +117,10 @@
             src = (shear, perm)[f - 4]
         return pltpu.make_async_copy(src, xb.at[f], in_sem.at[f])
 
+    own_basis = pltpu.make_async_copy(basis, own, in_sem.at[7])
+    own_basis.start()
     for f in ORDER:
         load(f).start()
-    own_basis = pltpu.make_async_copy(basis, bas.at[rad], in_sem.at[7])
-    own_basis.start()
     src_load = pltpu.make_async_copy(source, xb.at[6], in_sem.at[6])
     src_load.start()
 
@@ -128,7 +128,17 @@
     partners = near_peers + far_peers + [(az_up, rad), (az_dn, rad)]
     for peer in partners:
         pl.semaphore_signal(barrier, inc=1, device_id=peer, device_id_type=MESH)
+    own_basis.wait()
+    values, scale = encode(own[...].reshape(BR // 8, 8, NM))
+    code[pl.ds(0, BR), :] = values.reshape(BR, NM)
+    code[pl.ds(BR, 16), :] = jnp.concatenate([scale, scale], axis=0)
     pl.semaphore_wait(barrier, len(partners))
+
+    b_across = remote(code, bas.at[rad], bs.at[1], br_.at[1], (az, across))
+    b_mate = remote(code, bas.at[rad], bs.at[0], br_.at[0], (az, mate))
+    b_relay = remote(bas.at[across], bas.at[across], bs.at[2], br_.at[2], (az, mate))
+    b_across.start()
+    b_mate.start()
 
     lane = lax.broadcasted_iota(jnp.int32, (BA, BR), 1)
     zero_row = jnp.zeros((ROW, BR), F32)
@@ -160,14 +170,9 @@
             c.start()
         halo[f] = one
 
-    for f in ORDER[:5]:
+    for f in ORDER:
         stage_field(f)
 
-    b_across = remote(basis, bas.at[rad], bs.at[1], br_.at[1], (az, across))
-    b_mate = remote(basis, bas.at[rad], bs.at[0], br_.at[0], (az, mate))
-    b_relay = remote(bas.at[across], bas.at[across], bs.at[2], br_.at[2], (az, mate))
-    b_across.start()
-    b_mate.start()
 
     even = lax.rem(lane, 2) == 0
 
@@ -187,22 +192,24 @@
 
         lax.fori_loop(0, NH, place, 0, unroll=8)
 
-    def split_basis(j):
-        hi, lo = split(bas[j])
+    def split_basis(j, block):
+        hi, lo = split(block)
         rows = pl.ds(pl.multiple_of(j * BR, BR), BR)
         bhi[rows, :] = hi
         blo[rows, :] = lo
 
-    own_basis.wait()
-    split_basis(rad)
+    def decode_basis(j):
+        values = bas[j, pl.ds(0, BR)].astype(F32).reshape(BR // 8, 8, NM)
+        scale = bas[j, pl.ds(BR, 16)].astype(F32)[:8]
+        split_basis(j, decode(values, scale).reshape(BR, NM))
+
+    split_basis(rad, own[...])
     level = (lax.broadcasted_iota(jnp.int32, (LV, NM), 0) + LV * rad).astype(F32)
     half = jnp.sin(level * (math.pi / (2.0 * NH)))
     sigma = STORAGE + eigen[...] + 4.0 * half * half
     root = jnp.sqrt(sigma * (sigma + 4.0))
     lam = 2.0 / (sigma + 2.0 + root)
     inv_root = 1.0 / root
-    for f in ORDER[:4]:
-        finish_halo(f)
 
     lane3 = lax.broadcasted_iota(jnp.int32, (HB, CA, BR), 2)
     first = lane3 == 0
@@ -229,31 +236,44 @@
 
     src_load.wait()
 
-    def fluid_chunk(c, rr):
-        def rows(b, rr):
+    def fluid_rows(c, carry):
+        def rows(b, carry):
             h0 = b * HB
-            k, ks = neighbours(5, h0, c)
-            p, ps = neighbours(3, h0, c)
-            total = jnp.zeros_like(p)
-            for axis in range(3):
-                for side in range(2):
-                    total = total + (k + ks[axis][side]) * (p - ps[axis][side])
-            u0 = block(0, h0, c)
-            up, down = radial_pair(0, h0, c, u0)
-            spread = up - down
+            k = block(5, h0, c)
+            p = block(3, h0, c)
+            total = jnp.where(last, 0.0, k + pltpu.roll(k, BR - 1, 2)) * (p - pltpu.roll(p, BR - 1, 2))
+            total = total + jnp.where(first, 0.0, k + pltpu.roll(k, 1, 2)) * (p - pltpu.roll(p, 1, 2))
+            for move in (dict(dh=1), dict(dh=-1), dict(da=1), dict(da=-1)):
+                total = total + (k + block(5, h0, c, **move)) * (p - block(3, h0, c, **move))
+            u = block(0, h0, c)
+            spread = jnp.where(last, 0.0, pltpu.roll(u, BR - 1, 2)) - jnp.where(first, 0.0, pltpu.roll(u, 1, 2))
             spread = spread + (block(1, h0, c, da=1) - block(1, h0, c, da=-1))
             spread = spread + (block(2, h0, c, dh=1) - block(2, h0, c, dh=-1))
             s = xb[6, pl.ds(h0, HB), pl.ds(pl.multiple_of(CA * c, CA), CA), :].astype(F32)
             res = s + (0.5 * BIOT) * spread + STORAGE * p + 0.5 * total
-            tmp[pl.ds(pl.multiple_of(h0 * CA, CA), HB * CA), :] = res.reshape(HB * CA, BR)
-            return rr + jnp.sum(res * res, axis=0)
-
-        rr = lax.fori_loop(0, NH // HB, rows, rr, unroll=4)
+            tmp[c, pl.ds(pl.multiple_of(h0 * CA, CA), HB * CA), :] = res.reshape(HB * CA, BR)
+            return carry
+
+        return lax.fori_loop(0, NH // HB, rows, carry, unroll=8)
+
+    edge = lax.broadcasted_iota(jnp.int32, (CA, BR), 1)
+    edge = (edge == 0) | (edge == BR - 1)
+
+    def fluid_send(c, rr):
+        tile = cor[pl.ds(pl.multiple_of(CA * c, CA), CA), :]
+
+        def ends(h, rr):
+            rows = pl.ds(pl.multiple_of(h * CA, CA), CA)
+            res = tmp[c, rows, :] + jnp.where(edge, pltpu.roll(tile, 127 - 2 * h, 1), 0.0)
+            tmp[c, rows, :] = res
+            return rr + res * res
+
+        rr = lax.fori_loop(0, NH, ends, rr, unroll=8)
         table = fwd_tab[...]
         for pair in range(CA // 2):
             cols = []
             for i in range(2):
-                x = tmp[pl.ds(2 * pair + i, NH, stride=CA), :]
+                x = tmp[c, pl.ds(2 * pair + i, NH, stride=CA), :]
                 hi, lo = split(x)
                 cols.append(jnp.concatenate([hi, hi, lo], axis=0))
             y = dot(table, jnp.concatenate(cols, axis=1))
@@ -269,14 +289,26 @@
         t = lax.rem(rad + d, NRAD)
         return remote(fs.at[t, c], fr.at[rad, c], fss.at[d, c], frs.at[d, c], (az, t))
 
-    rr = lax.fori_loop(0, NCH // 2, fluid_chunk, jnp.zeros((CA, BR), F32))
-    stage_field(ORDER[5])
+    lax.fori_loop(1, NCH - 1, fluid_rows, 0)
+    for f in ORDER[:4]:
+        finish_halo(f)
+    beside_k, beside_p, beside_u = pk[5], pk[3], pk[0]
+    cor[...] = 0.5 * (qs[5].astype(F32) + beside_k) * (qs[3].astype(F32) - beside_p) + (0.5 * BIOT) * jnp.where(
+        even, beside_u, -beside_u
+    )
+    rr = lax.fori_loop(1, NCH - 1, fluid_send, jnp.zeros((CA, BR), F32))
     b_mate.wait_recv()
-    split_basis(mate)
+    decode_basis(mate)
     b_across.wait_recv()
     b_relay.start()
-    split_basis(across)
-    rr = lax.fori_loop(NCH // 2, NCH, fluid_chunk, rr)
+    decode_basis(across)
+
+    def outer_chunk(n, rr):
+        c = n * (NCH - 1)
+        fluid_rows(c, 0)
+        return fluid_send(c, rr)
+
+    rr = lax.fori_loop(0, 2, outer_chunk, rr)
 
     for f in ORDER[4:]:
         finish_halo(f)
@@ -309,13 +341,13 @@
                 square = square + res * res
             return rr + jnp.sum(square, axis=0), rz + jnp.sum(square * inv, axis=0)
 
-        return lax.fori_loop(0, NH // HB, rows, carry, unroll=4)
+        return lax.fori_loop(0, NH // HB, rows, carry, unroll=8)
 
     quad = jnp.zeros((CA, BR), F32)
     quad = lax.fori_loop(0, EARLY, moment_chunk, (quad, quad))
 
     b_relay.wait_recv()
-    split_basis(mate + 2 - 4 * (mate // 2))
+    decode_basis(mate + 2 - 4 * (mate // 2))
 
     def fwd_chunk(c, carry):
         y, w, power = carry
@@ -470,7 +502,8 @@
         pltpu.VMEM((6, 2, NH, BR), BF16),
         pltpu.VMEM((6, 2, NH, BR), BF16),
         pltpu.VMEM((2, NH, BR), F32),
-        pltpu.VMEM((NH * CA, BR), F32),
+        pltpu.VMEM((NCH, NH * CA, BR), F32),
+        pltpu.VMEM((BA, BR), F32),
         pltpu.VMEM((CA, NH, BR), F32),
         pltpu.VMEM((NRAD, NCH, CA + 1, LV, BR), WIRE),
         pltpu.VMEM((NRAD, NCH, CA + 1, LV, BR), WIRE),
@@ -481,7 +514,9 @@
         pltpu.VMEM((CA * LV, NM), F32),
         pltpu.VMEM((NRAD, NCH, CA + 1, LV, BR), WIRE),
         pltpu.VMEM((NRAD, NCH, CA + 1, LV, BR), WIRE),
-        pltpu.VMEM((NRAD, BR, NM), F32),
+        pltpu.VMEM((BR, NM), F32),
+        pltpu.VMEM((BR + 16, NM), WIRE),
+        pltpu.VMEM((NRAD, BR + 16, NM), WIRE),
         pltpu.VMEM((NM, NM), BF16),
         pltpu.VMEM((NM, NM), BF16),
         pltpu.VMEM((2, LV, NM), F32),

time: 67.6 us -> 62.2 us (0.920)
  Pallas kernels: 64.6 us -> 59.2 us
    pallas_call x1, Pallas kernels: 64.6 us -> 59.2 us  [body(): pl.pallas_call(kernel, out_shape=(pltpu.VMEM((4 * NH * BA, BR), F32), jax...]
where the time goes in v5:
time: 62.2 us; the launch traced here: 62 us
  Pallas kernels  59.2 us (95%)
  other arithmetic  2.81 us (5%)
    pallas_call x1, Pallas kernels, body(): pl.pallas_call(kernel, out_shape=(pltpu.VMEM((4 * NH * BA, BR), F32), jax...  59.2 us
    convert_element_type x1, other arithmetic, body(): return (alpha[0, 0] * step).astype(BF16).reshape(4, NH, BA, BR)  2.81 us

profile of v5, /device:TPU:1, one launch (start us, length us, event | category | flops | bytes accessed | tf_op | source)
XLA Modules:
  0.0 62.0 jit_solution(3207601711165646489)
XLA Ops:
  0.0 59.2 %residual_step.1 = (f32[16384,128]{1,0:T(8,128)S(1)}, f32[1,1]{1,0:T(1,128)}) custom-call(bf16[4,64,64,128]{3,2,1,0:T(8,128)(2,1)} %state.1, bf16[64,64,128]{2,1,0:T(8,128)(2,1)} %source.1, bf16[64,64,128]{2,1,0:T(8,128)(2,1)} %shear.1, bf16[64,64,128]{2,1,0:T(8,128)(2,1)} %perm.1, f32[128,512]{1,0:T(8,128)} %basis.1, f32[1,512]{1,0:T(1,128)} %bitcast.3, ...), custom_call_target="tpu_custom_call" | custom-call | tf_op jit(solution)/shard_map/residual_step/pallas_call | solution.py:534
  59.2 2.8 %multiply_convert_fusion = bf16[16384,128]{1,0:T(8,128)(2,1)} fusion(f32[16384,128]{1,0:T(8,128)S(1)} %get-tuple-element.8, f32[]{:T(128)} %bitcast.1), kind=kLoop, calls=%fused_computation | loop fusion | flops 4194304 | bytes 12582916 | tf_op jit(solution)/shard_map/convert_element_type | solution.py:545

commit v6 on v5

--- a/solution.py
+++ b/solution.py
@@ -18,7 +18,7 @@
 NM = NRAD * BR
 CA = 16
 NCH = BA // CA
-HB = 2
+HB = 4
 ROW = 80
 PAD = 8
 EARLY = 2
@@ -176,12 +176,16 @@
 
     even = lax.rem(lane, 2) == 0
 
-    def finish_halo(f):
-        for c in halo[f]:
+    def finish_columns(f):
+        for c in halo[f][:2]:
             c.wait_recv()
         left = jnp.where(rad > 0, ql[f].astype(F32), 0.0)
         right = jnp.where(rad < NRAD - 1, qr[f].astype(F32), 0.0)
         pk[f] = jnp.where(even, pltpu.roll(right, BR - 1, 1), pltpu.roll(left, 1, 1))
+
+    def finish_rows(f):
+        for c in halo[f][2:]:
+            c.wait_recv()
         ah32[0] = ahr[f, 0].astype(F32)
         ah32[1] = ahr[f, 1].astype(F32)
 
@@ -218,6 +222,10 @@
     def block(f, h0, c, dh=0, da=0):
         return ext[f, pl.ds(h0 + 1 + dh, HB), pl.ds(PAD + CA * c + da, CA), :]
 
+    def column(f, h0, c):
+        planes = ext[f, pl.ds(h0, HB + 2), pl.ds(pl.multiple_of(PAD + CA * c, PAD), CA), :]
+        return planes[:HB], planes[1 : HB + 1], planes[2:]
+
     def radial_pair(f, h0, c, v):
         tile = pk[f, pl.ds(pl.multiple_of(CA * c, CA), CA), :]
         ends = jnp.stack([pltpu.roll(tile, 127 - 2 * (h0 + i), 1) for i in range(HB)])
@@ -226,10 +234,10 @@
         return up, down
 
     def neighbours(f, h0, c):
-        v = block(f, h0, c)
+        below, v, above = column(f, h0, c)
         up, down = radial_pair(f, h0, c, v)
         return v, (
-            (block(f, h0, c, dh=1), block(f, h0, c, dh=-1)),
+            (above, below),
             (block(f, h0, c, da=1), block(f, h0, c, da=-1)),
             (up, down),
         )
@@ -239,12 +247,14 @@
     def fluid_rows(c, carry):
         def rows(b, carry):
             h0 = b * HB
-            k = block(5, h0, c)
-            p = block(3, h0, c)
+            k_below, k, k_above = column(5, h0, c)
+            p_below, p, p_above = column(3, h0, c)
             total = jnp.where(last, 0.0, k + pltpu.roll(k, BR - 1, 2)) * (p - pltpu.roll(p, BR - 1, 2))
             total = total + jnp.where(first, 0.0, k + pltpu.roll(k, 1, 2)) * (p - pltpu.roll(p, 1, 2))
-            for move in (dict(dh=1), dict(dh=-1), dict(da=1), dict(da=-1)):
-                total = total + (k + block(5, h0, c, **move)) * (p - block(3, h0, c, **move))
+            total = total + (k + k_above) * (p - p_above)
+            total = total + (k + k_below) * (p - p_below)
+            for da in (1, -1):
+                total = total + (k + block(5, h0, c, da=da)) * (p - block(3, h0, c, da=da))
             u = block(0, h0, c)
             spread = jnp.where(last, 0.0, pltpu.roll(u, BR - 1, 2)) - jnp.where(first, 0.0, pltpu.roll(u, 1, 2))
             spread = spread + (block(1, h0, c, da=1) - block(1, h0, c, da=-1))
@@ -290,13 +300,15 @@
         return remote(fs.at[t, c], fr.at[rad, c], fss.at[d, c], frs.at[d, c], (az, t))
 
     lax.fori_loop(1, NCH - 1, fluid_rows, 0)
-    for f in ORDER[:4]:
-        finish_halo(f)
+    for f in ORDER[:3]:
+        finish_columns(f)
     beside_k, beside_p, beside_u = pk[5], pk[3], pk[0]
     cor[...] = 0.5 * (qs[5].astype(F32) + beside_k) * (qs[3].astype(F32) - beside_p) + (0.5 * BIOT) * jnp.where(
         even, beside_u, -beside_u
     )
     rr = lax.fori_loop(1, NCH - 1, fluid_send, jnp.zeros((CA, BR), F32))
+    for f in (3, 5, 1):
+        finish_rows(f)
     b_mate.wait_recv()
     decode_basis(mate)
     b_across.wait_recv()
@@ -310,8 +322,10 @@
 
     rr = lax.fori_loop(0, 2, outer_chunk, rr)
 
-    for f in ORDER[4:]:
-        finish_halo(f)
+    for f in (1, 2, 4):
+        finish_columns(f)
+    for f in (0, 2, 4):
+        finish_rows(f)
 
     def moment_chunk(c, carry):
         def rows(b, carry):
@@ -320,12 +334,12 @@
             g, gs_ = neighbours(4, h0, c)
             face = [[g + gs_[axis][side] for side in range(2)] for axis in range(3)]
             diag2 = (face[0][0] + face[0][1]) + (face[1][0] + face[1][1]) + (face[2][0] + face[2][1])
-            p = block(3, h0, c)
+            p_below, p, p_above = column(3, h0, c)
             up, down = radial_pair(3, h0, c, p)
             grads = (
                 up - down,
                 block(3, h0, c, da=1) - block(3, h0, c, da=-1),
-                block(3, h0, c, dh=1) - block(3, h0, c, dh=-1),
+                p_above - p_below,
             )
             inv = 1.0 / diag2
             square = jnp.zeros_like(p)

time: 62.2 us -> 61.5 us (0.989)
  Pallas kernels: 59.2 us -> 58.5 us
    pallas_call x1, Pallas kernels: 59.2 us -> 58.5 us  [body(): pl.pallas_call(kernel, out_shape=(pltpu.VMEM((4 * NH * BA, BR), F32), jax...]
where the time goes in v6:
time: 61.5 us; the launch traced here: 61.3 us
  Pallas kernels  58.5 us (95%)
  other arithmetic  2.81 us (5%)
    pallas_call x1, Pallas kernels, body(): pl.pallas_call(kernel, out_shape=(pltpu.VMEM((4 * NH * BA, BR), F32), jax...  58.5 us
    convert_element_type x1, other arithmetic, body(): return (alpha[0, 0] * step).astype(BF16).reshape(4, NH, BA, BR)  2.81 us

profile of v6, /device:TPU:1, one launch (start us, length us, event | category | flops | bytes accessed | tf_op | source)
XLA Modules:
  0.0 61.3 jit_solution(12424380213880822498)
XLA Ops:
  0.0 58.5 %residual_step.1 = (f32[16384,128]{1,0:T(8,128)S(1)}, f32[1,1]{1,0:T(1,128)}) custom-call(bf16[4,64,64,128]{3,2,1,0:T(8,128)(2,1)} %state.1, bf16[64,64,128]{2,1,0:T(8,128)(2,1)} %source.1, bf16[64,64,128]{2,1,0:T(8,128)(2,1)} %shear.1, bf16[64,64,128]{2,1,0:T(8,128)(2,1)} %perm.1, f32[128,512]{1,0:T(8,128)} %basis.1, f32[1,512]{1,0:T(1,128)} %bitcast.3, ...), custom_call_target="tpu_custom_call" | custom-call | tf_op jit(solution)/shard_map/residual_step/pallas_call | solution.py:548
  58.5 2.8 %multiply_convert_fusion = bf16[16384,128]{1,0:T(8,128)(2,1)} fusion(f32[16384,128]{1,0:T(8,128)S(1)} %get-tuple-element.8, f32[]{:T(128)} %bitcast.1), kind=kLoop, calls=%fused_computation | loop fusion | flops 4194304 | bytes 12582916 | tf_op jit(solution)/shard_map/convert_element_type | solution.py:559
